TPU v7x, 32 devices: a whole 2x2x4 slice. The times are simulated.
32 devices in a mesh: section: 2 (over y), channel: 4 (over x, core), block: 4 (over z).
Axes of the slice: x: 2, y: 2, z: 4, core: 2. Of those that a mesh axis runs over, the one named last changes fastest.
Arguments:
- env: bfloat16 [2, 16, 16, 512, 512], P('section', 'channel', 'block'), may hold values from -6 to 6
- site_tensor: bfloat16 [2, 4, 16, 512, 512], P('section', None, 'block'), may hold values from -0.25 to 0.25
- mpo: bfloat16 [2, 16, 16, 4], P('section'), may hold values from -2 to 2
- channel_mask: int32 [2, 16, 16], P('section'), may hold values 0 or 1
- block_mask: int32 [2, 4, 16], P('section', None, 'block'), may hold values 0 or 1
- state_charge: int32 [4], replicated, may hold values from 0 to 1, as said below
- psi: bfloat16 [2, 16, 512, 512], P('section', 'block'), may hold values from -0.0014648438 to 0.0014648438
Outputs:
- new_env: bfloat16 [2, 16, 16, 512, 512], P('section', 'channel', 'block')
- new_psi: bfloat16 [512, 2, 16, 512], P('channel', 'section', 'block')
Inputs may be any that keep to these rules, and one draw needn't show every extreme that they name: `state_charge`: half of the 4 site states carry charge 0, the others charge 1.
All inputs are finite; a program needn't handle non-finite values. No bound on the sum of `channel_mask` or of `block_mask` on one device may be relied on, other than what follows from the above.
Results may differ from a plain program's by a relative error of at most 0.017.
Values may be sent and summed in bfloat16 or wider, within the bound.
No kernel may reach another device: no remote copies, remote signals or barrier semaphores. Data moves between devices by JAX's collectives and lax.ppermute only.
A program may use at most 192 MiB of HBM per device.

v0:
```python
import jax
import jax.numpy as jnp
from jax import lax
from jax.sharding import PartitionSpec as P


def padded(block, sides, width):
    for axis, dim in sides:
        count = lax.axis_size(axis)
        forward = [(i, i + 1) for i in range(count - 1)]
        backward = [(target, source) for source, target in forward]
        low = lax.ppermute(
            lax.slice_in_dim(block, block.shape[dim] - width, None, axis=dim), axis, forward
        )
        high = lax.ppermute(lax.slice_in_dim(block, 0, width, axis=dim), axis, backward)
        block = jnp.concatenate([low, block, high], axis=dim)
    return block


def from_partner(value, axis, bit):
    return lax.ppermute(value, axis, [(i, i ^ 1 << bit) for i in range(lax.axis_size(axis))])


def per_device(env, site_tensor, mpo, channel_mask, block_mask, state_charge, psi):
    section = lax.axis_index("section")
    own_env = env[0]
    site_blocks = site_tensor[0]
    weights = mpo[0] * channel_mask[0].astype(jnp.bfloat16)[:, :, None]
    chan_dev = own_env.shape[0]
    offset_w = lax.axis_index("channel") * chan_dev
    gathered = lax.all_gather(own_env, "channel", axis=0, tiled=True)
    local_w = lax.dynamic_slice_in_dim(weights, offset_w, chan_dev, 1)
    blended_environment = jnp.einsum(
        "wvs,wqab->vsqab", local_w, gathered, preferred_element_type=jnp.float32
    ).astype(jnp.bfloat16)
    product = jnp.einsum(
        "vsqac,sqcb->vsqab", blended_environment, site_blocks, preferred_element_type=jnp.float32
    ).astype(jnp.bfloat16)
    contracted_layers = jnp.einsum(
        "sqca,vsqcb->vsqab", site_blocks, product, preferred_element_type=jnp.float32
    )
    charge_label = state_charge.astype(jnp.float32)
    sector_present = block_mask[0].astype(jnp.float32)
    resident_part = jnp.einsum(
        "vsqab,sq->vqab", contracted_layers, sector_present * (1.0 - charge_label)[:, None]
    )
    outgoing_part = jnp.einsum(
        "vsqab,sq->vqab", contracted_layers, sector_present * charge_label[:, None]
    ).astype(jnp.bfloat16)
    rim_cells = padded(outgoing_part, (("block", 1),), 1)
    sector_count = outgoing_part.shape[1]
    shifted = jnp.where(section == 0, rim_cells[:, :sector_count], rim_cells[:, 2:])
    new_env = (resident_part + shifted.astype(jnp.float32)).astype(jnp.bfloat16)
    partner = from_partner(new_env, "section", 0)
    left_env = jnp.where(section == 0, new_env, partner)
    right_env = jnp.where(section == 0, partner, new_env)
    applied = jnp.einsum(
        "wqab,vqbd->wvqad", left_env, psi, preferred_element_type=jnp.float32
    ).astype(jnp.bfloat16)
    summed = lax.psum_scatter(
        jnp.einsum("wvqad,wqcd->avqc", applied, right_env, preferred_element_type=jnp.float32),
        "channel",
        scatter_dimension=0,
        tiled=True,
    )
    return (new_env[None], summed.astype(jnp.bfloat16))


def solution(mesh):
    return jax.shard_map(
        per_device,
        mesh=mesh,
        in_specs=(
            P("section", "channel", "block", None, None),
            P("section", None, "block", None, None),
            P("section", None, None, None),
            P("section", None, None),
            P("section", None, "block"),
            P(),
            P("section", "block", None, None),
        ),
        out_specs=(
            P("section", "channel", "block", None, None),
            P("channel", "section", "block", None),
        ),
        check_vma=False,
    )
```

profile of v0, /device:TPU:0, one launch (start us, length us, event | category | flops | bytes accessed | tf_op | source)
XLA Modules:
  0.0 681.7 jit_solution(10469324333053368263)
XLA Ops:
  7.3 0.7 all-gather.3.cloned.1.call-update
  8.0 0.1 constant_dynamic-slice_fusion
  8.1 0.1 fusion.31
  8.2 0.1 copy.16
  8.3 0.1 fusion.32
  8.4 205.4 %all-gather.3.cloned.1.call-done = bf16[1,16,4,512,512]{4,3,2,0,1:T(8,128)(2,1)} async-done(((bf16[1,4,4,512,512]{4,3,2,0,1:T(8,128)(2,1)}), bf16[1,16,4,512,512]{4,3,2,0,1:T(8,128)(2,1)}) %all-gather.3.cloned.1.call-update) | async-done | bytes 33554448 | tf_op jit(solution)/shard_map/all_gather | solution.py:31
  213.8 58.6 %fusion.6 = bf16[4,4,4,512,512]{4,1,3,2,0:T(4,128)(2,1)} fusion(bf16[16,4,4,1,1]{0,2,4,3,1:T(4,128)(2,1)S(1)} %copy.16, bf16[16,4,512,512,1]{3,2,1,0,4:T(8,128)(2,1)} %bitcast.85), kind=kOutput, calls=%fused_computation.9 | convolution fusion | flops 536870912 | bytes 67109376 | tf_op jit(solution)/shard_map/wvs,wqab->vsqab/dot_general | solution.py:33
  272.5 35.8 %fusion.3.clone.4 = bf16[4,4,4,512,512]{3,4,0,2,1:T(8,128)(2,1)} fusion(bf16[1,4,4,512,512]{4,3,2,1,0:T(8,128)(2,1)} %param.8, bf16[4,4,4,512,512]{4,1,3,2,0:T(4,128)(2,1)} %fusion.6), kind=kOutput, calls=%fused_computation.6.clone.clone.clone.1 | convolution fusion | flops 17196646400 | bytes 75497472 | tf_op jit(solution)/shard_map/vsqac,sqcb->vsqab/dot_general | solution.py:36
  308.3 36.8 %fusion.1 = (bf16[4,4,512,512]{2,3,1,0:T(8,128)(2,1)}, f32[4,4,512,512]{2,3,1,0:T(8,128)}) fusion(f32[4,4]{0,1:T(4,128)S(1)} %get-tuple-element.11, f32[4,4]{0,1:T(4,128)S(1)} %get-tuple-element.10, bf16[1,4,4,512,512]{4,3,2,1,0:T(8,128)(2,1)} %param.8, bf16[4,4,4,512,512]{3,4,0,2,1:T(8,128)(2,1)} %fusion.3.clone.4), kind=kOutput, calls=%fused_computation.3 | convolution fusion | flops 17238589440 | bytes 67108992 | tf_op jit(solution)/shard_map/sqca,vsqcb->vsqab/dot_general | solution.py:39
  345.1 13.3 %copy.34 = bf16[4,4,512,512]{3,2,0,1:T(8,128)(2,1)} copy(bf16[4,4,512,512]{2,3,1,0:T(8,128)(2,1)} %get-tuple-element.6) | data formatting | bytes 16777216 | tf_op jit(solution)/shard_map/vsqab,sq->vqab/dot_general | solution.py:47
  358.4 4.5 fusion.34
  362.9 4.7 collective-permute-start
  367.6 1.3 collective-permute-start.1
  368.9 19.2 %copy.27 = f32[4,4,512,512]{3,2,0,1:T(8,128)} copy(f32[4,4,512,512]{2,3,1,0:T(8,128)} %get-tuple-element.7) | data formatting | bytes 33554432 | tf_op jit(solution)/shard_map/vsqab,sq->vqab/dot_general | solution.py:44
  388.1 23.8 %collective-permute-done = bf16[4,1,512,512]{3,2,1,0:T(8,128)(2,1)} collective-permute-done((bf16[4,1,512,512]{3,2,1,0:T(8,128)(2,1)}, bf16[4,1,512,512]{3,2,1,0:T(8,128)(2,1)}, u32[]{:S(2)}, u32[]{:S(2)}) %collective-permute-start) | collective-permute-done | bytes 2097184 | tf_op jit(solution)/shard_map/ppermute | solution.py:12
  411.9 5.4 collective-permute-done.1
  417.3 11.3 %fusion.13 = bf16[4,4,512,512]{3,2,1,0:T(8,128)(2,1)S(1)} fusion(f32[4,4,512,512]{3,2,0,1:T(8,128)} %copy.27, bf16[4,1,512,512]{3,2,1,0:T(8,128)(2,1)} %collective-permute-done.1, bf16[4,4,512,512]{3,2,1,0:T(8,128)(2,1)} %bitcast.84, bf16[4,1,512,512]{3,2,1,0:T(8,128)(2,1)} %collective-permute-done, pred[]{:T(512)S(6)} %eq.2), kind=kLoop, calls=%fused_computation.13 | loop fusion | flops 25165824 | bytes 37748736 | tf_op jit(solution)/shard_map/convert_element_type | solution.py:53
  428.7 1.5 collective-permute-start.2
  430.2 180.1 %collective-permute-done.2 = bf16[4,4,512,512]{3,2,1,0:T(8,128)(2,1)} collective-permute-done((bf16[4,4,512,512]{3,2,1,0:T(8,128)(2,1)S(1)}, bf16[4,4,512,512]{3,2,1,0:T(8,128)(2,1)}, u32[]{:S(2)}, u32[]{:S(2)}) %collective-permute-start.2) | collective-permute-done | bytes 8388640 | tf_op jit(solution)/shard_map/ppermute | solution.py:21
  610.3 6.7 convert_bitcast_fusion
  617.0 10.8 %fusion.25 = f32[512,1,4,512]{0,3,2,1:T(8,128)} fusion(bf16[4,4,512,512]{3,2,0,1:T(8,128)(2,1)} %convert_bitcast_fusion, bf16[4,4,512,512]{3,2,1,0:T(8,128)(2,1)} %collective-permute-done.2, bf16[4,4,512,512]{3,2,1,0:T(8,128)(2,1)} %copy-done.1, pred[]{:T(512)S(6)} %eq.2), kind=kOutput, calls=%fused_computation.27 | convolution fusion | flops 4299161600 | bytes 29360128 | tf_op jit(solution)/shard_map/wvqad,wqcd->avqc/dot_general | solution.py:61
  627.9 44.5 %reduce-scatter.2.cloned.1.call-done = f32[128,1,4,512]{0,3,2,1:T(8,128)} async-done(((f32[512,1,4,512]{0,3,2,1:T(8,128)}), f32[128,1,4,512]{0,3,2,1:T(8,128)}) %reduce-scatter.2.cloned.1.call-update) | async-done | bytes 1048592 | tf_op jit(solution)/shard_map/reduce_scatter | solution.py:60
  672.3 1.3 convert_element_type.71
  673.6 1.2 copy.15
  (18 shorter events, 0.2 us)
Async XLA Ops:
  7.2 603.1 %copy-start = (bf16[1,4,512,512]{3,2,1,0:T(8,128)(2,1)S(1)}, bf16[1,4,512,512]{3,2,1,0:T(8,128)(2,1)}, u32[]{:S(2)}) copy-start(bf16[1,4,512,512]{3,2,1,0:T(8,128)(2,1)} %param.13) | copy-start | bytes 6291460
  7.2 0.8 copy-start.3
  7.2 0.9 copy-start.2
  7.2 1.1 copy-start.5
  7.2 1.1 copy-start.4
  7.2 206.6 %all-gather.3.cloned.1.call-start = ((), (), s32[]{:S(2)}) async-start(), calls=%async_computation.2 | async-start | bytes 41943040 | tf_op jit(solution)/shard_map/all_gather | solution.py:31
  8.0 664.4 %reduce-scatter.2.cloned.1.call-start = ((), (), s32[]{:S(2)}) async-start(), calls=%async_computation.1 | async-start | bytes 5242880 | tf_op jit(solution)/shard_map/reduce_scatter | solution.py:60
  362.9 49.0 %collective-permute-start = (bf16[4,1,512,512]{3,2,1,0:T(8,128)(2,1)}, bf16[4,1,512,512]{3,2,1,0:T(8,128)(2,1)}, u32[]{:S(2)}, u32[]{:S(2)}) collective-permute-start(bf16[4,1,512,512]{3,2,1,0:T(8,128)(2,1)} %get-tuple-element.8), channel_id=1, source_target_pairs={{0,1},{1,2},{2,3},{4,5},{5,6},{6,7},{8,9},{9,10},{10,11},{12,13},{... | collective-permute-start | bytes 6291464 | tf_op jit(solution)/shard_map/ppermute | solution.py:12
  367.6 49.7 %collective-permute-start.1 = (bf16[4,1,512,512]{3,2,1,0:T(8,128)(2,1)}, bf16[4,1,512,512]{3,2,1,0:T(8,128)(2,1)}, u32[]{:S(2)}, u32[]{:S(2)}) collective-permute-start(bf16[4,1,512,512]{3,2,1,0:T(8,128)(2,1)} %get-tuple-element.9), channel_id=1, source_target_pairs={{1,0},{2,1},{3,2},{5,4},{6,5},{7,6},{9,8},{10,9},{11,10},{13,12},{... | collective-permute-start | bytes 6291464 | tf_op jit(solution)/shard_map/ppermute | solution.py:15
  428.7 181.7 %copy-start.1 = (bf16[4,4,512,512]{3,2,1,0:T(8,128)(2,1)}, bf16[4,4,512,512]{3,2,1,0:T(8,128)(2,1)S(1)}, u32[]{:S(2)}) copy-start(bf16[4,4,512,512]{3,2,1,0:T(8,128)(2,1)S(1)} %fusion.13) | copy-start | bytes 25165828
  428.7 181.6 %collective-permute-start.2 = (bf16[4,4,512,512]{3,2,1,0:T(8,128)(2,1)S(1)}, bf16[4,4,512,512]{3,2,1,0:T(8,128)(2,1)}, u32[]{:S(2)}, u32[]{:S(2)}) collective-permute-start(bf16[4,4,512,512]{3,2,1,0:T(8,128)(2,1)S(1)} %fusion.13), channel_id=1, source_target_pairs={{0,16},{16,0},{1,17},{17,1},{2,18},{18,2},{3,19},{19,3},{4,20},{20... | collective-permute-start | bytes 25165832 | tf_op jit(solution)/shard_map/ppermute | solution.py:21
Sparse Core Ops, SparseCore 0:
  9.6 204.2 all-gather.2
  628.0 44.3 reduce-scatter.1
where the time goes:
time: 683 us; the launch traced here: 682 us
  waiting for transfers between devices  460 us (67%)
  matrix products  149 us (22%)
  local copies, waits for them, and re-layouts  38.5 us (6%)
  between operations  14.1 us (2%)
  other arithmetic  12.8 us (2%)
  starting transfers between devices  7.6 us (1%)
    all_gather x1, waiting for transfers between devices, per_device(): gathered = lax.all_gather(own_env, 'channel', axis=0, tiled=True)  205 us
    ppermute x1, waiting for transfers between devices, from_partner(): lax.ppermute(value, axis, [(i, i ^ 1 << bit) for i in range(lax.axis_size...  180 us
    dot_general x1, matrix products, per_device(): jnp.einsum('wvs,wqab->vsqab', local_w, gathered, preferred_element_type=j...  58.6 us
    reduce_scatter x1, waiting for transfers between devices, per_device(): lax.psum_scatter(jnp.einsum('wvqad,wqcd->avqc', applied, right_env, prefe...  44.5 us
    dot_general x1, matrix products, per_device(): jnp.einsum('sqca,vsqcb->vsqab', site_blocks, product, preferred_element_t...  36.8 us
    dot_general x1, matrix products, per_device(): jnp.einsum('vsqac,sqcb->vsqab', blended_environment, site_blocks, preferr...  35.8 us
    ppermute x1, waiting for transfers between devices, padded(): lax.ppermute(lax.slice_in_dim(block, block.shape[dim] - width, None, axis...  23.8 us
    dot_general x1, local copies, waits for them, and re-layouts, per_device(): jnp.einsum('vsqab,sq->vqab', contracted_layers, sector_present * (1.0 - c...  19.2 us
  transfers between devices with their start and end apart: 5, of which 5 were waited for; matrix products, arithmetic and copies ran while one was open for 3% of the time, Pallas kernels for 0%

commit v1 on v0

v1 whole, which is shorter than its diff:
```python
import functools

import jax
import jax.numpy as jnp
from jax import lax
from jax.experimental import pallas as pl
from jax.experimental.pallas import tpu as pltpu
from jax.sharding import PartitionSpec as P


ROWS = 16
F32 = jnp.float32
BF16 = jnp.bfloat16


def padded(block, sides, width):
    for axis, dim in sides:
        count = lax.axis_size(axis)
        forward = [(i, i + 1) for i in range(count - 1)]
        backward = [(target, source) for source, target in forward]
        low = lax.ppermute(
            lax.slice_in_dim(block, block.shape[dim] - width, None, axis=dim), axis, forward
        )
        high = lax.ppermute(lax.slice_in_dim(block, 0, width, axis=dim), axis, backward)
        block = jnp.concatenate([low, block, high], axis=dim)
    return block


def from_partner(value, axis, bit):
    return lax.ppermute(value, axis, [(i, i ^ 1 << bit) for i in range(lax.axis_size(axis))])


def general_plan(env, site_tensor, mpo, channel_mask, block_mask, state_charge, psi):
    section = lax.axis_index("section")
    own_env = env[0]
    site_blocks = site_tensor[0]
    weights = mpo[0] * channel_mask[0].astype(BF16)[:, :, None]
    chan_dev = own_env.shape[0]
    offset_w = lax.axis_index("channel") * chan_dev
    gathered = lax.all_gather(own_env, "channel", axis=0, tiled=True)
    local_w = lax.dynamic_slice_in_dim(weights, offset_w, chan_dev, 1)
    blended = jnp.einsum(
        "wvs,wqab->vsqab", local_w, gathered, preferred_element_type=F32
    ).astype(BF16)
    product = jnp.einsum(
        "vsqac,sqcb->vsqab", blended, site_blocks, preferred_element_type=F32
    ).astype(BF16)
    layers = jnp.einsum("sqca,vsqcb->vsqab", site_blocks, product, preferred_element_type=F32)
    charge_label = state_charge.astype(F32)
    present = block_mask[0].astype(F32)
    resident = jnp.einsum("vsqab,sq->vqab", layers, present * (1.0 - charge_label)[:, None])
    outgoing = jnp.einsum("vsqab,sq->vqab", layers, present * charge_label[:, None]).astype(BF16)
    rim_cells = padded(outgoing, (("block", 1),), 1)
    sector_count = outgoing.shape[1]
    shifted = jnp.where(section == 0, rim_cells[:, :sector_count], rim_cells[:, 2:])
    new_env = (resident + shifted.astype(F32)).astype(BF16)
    partner = from_partner(new_env, "section", 0)
    left_env = jnp.where(section == 0, new_env, partner)
    right_env = jnp.where(section == 0, partner, new_env)
    applied = jnp.einsum(
        "wqab,vqbd->wvqad", left_env, psi, preferred_element_type=F32
    ).astype(BF16)
    summed = lax.psum_scatter(
        jnp.einsum("wvqad,wqcd->avqc", applied, right_env, preferred_element_type=F32),
        "channel",
        scatter_dimension=0,
        tiled=True,
    )
    return (new_env[None], summed.astype(BF16))


def dot_nn(a, b):
    return lax.dot_general(a, b, (((1,), (0,)), ((), ())), preferred_element_type=F32)


def dot_nt(a, b):
    return lax.dot_general(a, b, (((1,), (1,)), ((), ())), preferred_element_type=F32)


def sector_body(pieces_n, has_prev, has_hold, strips, sc, *refs):
    pieces = refs[:pieces_n]
    mixer, site, site_t = refs[pieces_n : pieces_n + 3]
    rest = list(refs[pieces_n + 3 :])
    prev = rest.pop(0) if has_prev else None
    hold = rest.pop(0) if has_hold else None
    first_out, second_out, mixed, prod = rest
    chan, strip, dim = pieces[0].shape
    states = site.shape[0]
    half = states // 2
    step = pl.program_id(0)

    @pl.when(step < strips)
    def _():
        for group in range(strip // ROWS):
            rows = pl.ds(group * ROWS, ROWS)
            slab = [p[:, rows, :].reshape(chan * ROWS, dim) for p in pieces]
            out = dot_nn(mixer[...], jnp.concatenate(slab, axis=0)).astype(BF16)
            mixed[:, rows, :] = out.reshape(states * chan, ROWS, dim)
        for at in range(states):
            side, k = divmod(at, half)
            left = mixed[at * chan : (at + 1) * chan].reshape(chan * strip, dim)
            out = dot_nn(left, site[sc[1 + at], 0]).astype(BF16).reshape(chan, strip, dim)
            rows = pl.ds(pl.multiple_of(k * dim + step * strip, strip), strip)
            prod[side * chan : (side + 1) * chan, rows, :] = out

    @pl.when(step >= strips)
    def _():
        v = step - strips

        def total(side):
            left = [site_t[sc[1 + side * half + k], 0] for k in range(half)]
            return dot_nn(jnp.concatenate(left, axis=1), prod[side * chan + v])

        stay = total(0)
        if has_prev:
            first_out[0] = (stay + prev[0].astype(F32)).astype(BF16)
        else:
            first_out[0] = stay
        moving = total(1).astype(BF16)
        if has_hold:
            second_out[0] = (hold[0] + moving.astype(F32)).astype(BF16)
        else:
            second_out[0] = moving


def sector_step(scalars, pieces, mixer, site, site_t, prev=None, hold=None):
    chan, dim, _ = pieces[0].shape
    states = site.shape[0]
    strip = 128
    strips = dim // strip
    by_chan = pl.BlockSpec((1, dim, dim), lambda i, sc: (jnp.maximum(i - strips, 0), 0, 0))
    in_specs = [
        pl.BlockSpec((chan, strip, dim), lambda i, sc: (0, jnp.minimum(i, strips - 1), 0))
        for _ in pieces
    ]
    in_specs += [
        pl.BlockSpec(mixer.shape, lambda i, sc: (0, 0)),
        pl.BlockSpec((states, 1, dim, dim), lambda i, sc: (0, sc[0], 0, 0)),
        pl.BlockSpec((states, 1, dim, dim), lambda i, sc: (0, sc[0], 0, 0)),
    ]
    extra = [x for x in (prev, hold) if x is not None]
    in_specs += [by_chan for _ in extra]
    body = functools.partial(sector_body, len(pieces), prev is not None, hold is not None, strips)
    flops = 2 * dim**3 * chan * states * 2 + 2 * dim * dim * mixer.shape[0] * len(pieces) * chan
    return pl.pallas_call(
        body,
        grid_spec=pltpu.PrefetchScalarGridSpec(
            num_scalar_prefetch=1,
            grid=(strips + chan,),
            in_specs=in_specs,
            out_specs=[by_chan, by_chan],
            scratch_shapes=[
                pltpu.VMEM((states * chan, strip, dim), BF16),
                pltpu.VMEM((2 * chan, states // 2 * dim, dim), BF16),
            ],
        ),
        out_shape=[
            jax.ShapeDtypeStruct((chan, dim, dim), F32 if prev is None else BF16),
            jax.ShapeDtypeStruct((chan, dim, dim), BF16),
        ],
        compiler_params=pltpu.CompilerParams(dimension_semantics=("arbitrary",)),
        cost_estimate=pl.CostEstimate(
            flops=flops, transcendentals=0, bytes_accessed=2 * dim * dim * chan * 10
        ),
    )(scalars, *pieces, mixer, site, site_t, *extra)


def ready_body(sc, other, vecs, out):
    @pl.when(sc[0] == 0)
    def _():
        for n in range(vecs.shape[0]):
            out[n, 0] = dot_nt(vecs[n], other[0]).astype(BF16)

    @pl.when(sc[0] != 0)
    def _():
        for n in range(vecs.shape[0]):
            out[n, 0] = dot_nn(other[0], vecs[n]).astype(BF16)


def ready_step(section, other, vecs):
    chan, dim, _ = other.shape
    count = vecs.shape[0]
    return pl.pallas_call(
        ready_body,
        grid_spec=pltpu.PrefetchScalarGridSpec(
            num_scalar_prefetch=1,
            grid=(chan,),
            in_specs=[
                pl.BlockSpec((1, dim, dim), lambda i, sc: (i, 0, 0)),
                pl.BlockSpec((count, dim, dim), lambda i, sc: (0, 0, 0)),
            ],
            out_specs=pl.BlockSpec((count, 1, dim, dim), lambda i, sc: (0, i, 0, 0)),
        ),
        out_shape=jax.ShapeDtypeStruct((count, chan, dim, dim), BF16),
        compiler_params=pltpu.CompilerParams(dimension_semantics=("arbitrary",)),
        cost_estimate=pl.CostEstimate(
            flops=2 * dim**3 * chan * count, transcendentals=0, bytes_accessed=2 * dim * dim * chan * 3
        ),
    )(section, other, vecs)


def apply_body(sc, own, ready, keep, send, acc):
    chan = own.shape[0]
    slots = 2 * keep.shape[0]
    rows = keep.shape[-2]

    @pl.when(sc[0] == 0)
    def _():
        total = dot_nn(own[0], ready[0, 0])
        for w in range(1, chan):
            total += dot_nn(own[w], ready[0, w])
        acc[...] = total

    @pl.when(sc[0] != 0)
    def _():
        total = dot_nt(ready[0, 0], own[0])
        for w in range(1, chan):
            total += dot_nt(ready[0, w], own[w])
        acc[...] = total

    for j in range(slots):
        start = pl.multiple_of((sc[1] ^ j) * rows, rows)
        value = acc[pl.ds(start, rows), :]
        if j % 2:
            send[j // 2, 0] = value.astype(BF16)
        else:
            keep[j // 2, 0] = value


def apply_step(scalars, own, ready, slots):
    chan, dim, _ = own.shape
    count = ready.shape[0]
    shape = (slots // 2, count, dim // slots, dim)
    spec = pl.BlockSpec((slots // 2, 1, dim // slots, dim), lambda n, sc: (0, n, 0, 0))
    return pl.pallas_call(
        apply_body,
        grid_spec=pltpu.PrefetchScalarGridSpec(
            num_scalar_prefetch=1,
            grid=(count,),
            in_specs=[
                pl.BlockSpec((chan, dim, dim), lambda n, sc: (0, 0, 0)),
                pl.BlockSpec((1, chan, dim, dim), lambda n, sc: (n, 0, 0, 0)),
            ],
            out_specs=[spec, spec],
            scratch_shapes=[pltpu.VMEM((dim, dim), F32)],
        ),
        out_shape=[jax.ShapeDtypeStruct(shape, F32), jax.ShapeDtypeStruct(shape, BF16)],
        compiler_params=pltpu.CompilerParams(dimension_semantics=("arbitrary",)),
        cost_estimate=pl.CostEstimate(
            flops=2 * dim**3 * chan * count, transcendentals=0, bytes_accessed=2 * dim * dim * chan * 3
        ),
    )(scalars, own, ready)


def place_body(sc, *refs):
    out = refs[-1]
    for u, part in enumerate(refs[:-1]):
        out[0, pl.ds(sc[u], 1)] = part[...]


def place_step(slots, parts):
    chan, dim, _ = parts[0].shape
    return pl.pallas_call(
        place_body,
        grid_spec=pltpu.PrefetchScalarGridSpec(
            num_scalar_prefetch=1,
            grid=(chan,),
            in_specs=[pl.BlockSpec((1, dim, dim), lambda i, sc: (i, 0, 0)) for _ in parts],
            out_specs=pl.BlockSpec((1, len(parts), dim, dim), lambda i, sc: (i, 0, 0, 0)),
        ),
        out_shape=jax.ShapeDtypeStruct((chan, len(parts), dim, dim), parts[0].dtype),
        compiler_params=pltpu.CompilerParams(dimension_semantics=("arbitrary",)),
    )(slots, *parts)


def swap(value, axis, bit=0):
    return lax.ppermute(value, axis, [(i, i ^ (1 << bit)) for i in range(lax.axis_size(axis))])


def pick(array, index, axis):
    return lax.dynamic_index_in_dim(array, index, axis, keepdims=False)


def sector_order(sectors):
    return [sectors - 1] + list(range(sectors - 1))


def pipelined_plan(env, site_tensor, mpo, channel_mask, block_mask, state_charge, psi):
    section = lax.axis_index("section")
    me = lax.axis_index("channel")
    peers = lax.axis_size("channel")
    bits = peers.bit_length() - 1
    blocks = lax.axis_size("block")
    own_env = env[0]
    chan, sectors, _, _ = own_env.shape
    site = site_tensor[0]
    states = site.shape[0]

    def sector(u):
        return jnp.where(section == 0, u, sectors - 1 - u)

    order = sector_order(sectors)

    gathered = {}
    for u in order:
        pieces = {0: lax.optimization_barrier(pick(own_env, sector(u), 1))}
        for bit in reversed(range(bits)):
            moved = {}
            for j, p in pieces.items():
                moved[j | 1 << bit] = swap(p, "channel", bit)
            pieces.update(moved)
        gathered[u] = [pieces[j] for j in range(peers)]

    upper = range(sectors // 2, sectors)
    vecs = {}
    for u in upper:
        mine = pick(psi[0], sector(u), 0)
        theirs = swap(pick(psi[0], sector(sectors - 1 - u), 0), "section")
        vecs[u] = jnp.stack([mine, theirs])

    inputs = peers * chan
    outputs = states * chan
    key = state_charge * states + jnp.arange(states, dtype=jnp.int32)
    rank = jnp.sum((key[None, :] < key[:, None]).astype(jnp.int32), axis=1)
    chosen = rank[None, :] == jnp.arange(states, dtype=jnp.int32)[:, None]
    state_ids = jnp.arange(states, dtype=jnp.int32)[None, :]
    state_order = jnp.sum(jnp.where(chosen, state_ids, 0), axis=1)
    weights = mpo[0].astype(F32) * channel_mask[0].astype(F32)[:, :, None]
    weights = lax.dynamic_slice_in_dim(weights, me * chan, chan, 1)
    weights = weights.reshape(peers, chan, chan, states)
    weights = jnp.stack([pick(weights, me ^ j, 0) for j in range(peers)])
    weights = weights.reshape(inputs, chan, states)
    out_row = jnp.arange(outputs * ROWS)[:, None]
    in_row = jnp.arange(inputs * ROWS)[None, :]
    spread_out = (out_row // ROWS == jnp.arange(outputs)[None, :]).astype(BF16)
    spread_in = (in_row // ROWS == jnp.arange(inputs)[:, None]).astype(BF16)
    same_row = out_row % ROWS == in_row % ROWS
    site_t = jnp.swapaxes(site, 2, 3)

    def mixer(u):
        present = pick(block_mask[0], sector(u), 1).astype(F32)
        by_state = jnp.moveaxis(weights * present, 2, 0)
        picked = jnp.where(chosen[:, :, None, None], by_state[None], 0.0)
        table = jnp.swapaxes(jnp.sum(picked, axis=1), 1, 2).reshape(outputs, inputs)
        wide = spread_out @ table.astype(BF16) @ spread_in
        return jnp.where(same_row, wide, 0).astype(BF16)

    def scalars(u):
        return jnp.concatenate([sector(u)[None], state_order]).astype(jnp.int32)

    def step(u, *extra):
        return sector_step(scalars(u), gathered[u], mixer(u), site, site_t, *extra)

    links = [(b, b + 1) for b in range(blocks - 1)]
    links += [(blocks + b + 1, blocks + b) for b in range(blocks - 1)]

    new = {}
    last = sectors - 1
    hold, moving = step(last)
    raised = lax.ppermute(moving, ("section", "block"), links)
    for u in range(last):
        final = hold if u == last - 1 else None
        new[u], moving = step(u, moving if u else None, final)
        if u == 0:
            new[0] = (new[0] + raised.astype(F32)).astype(BF16)
    new[last] = moving

    flag = section.astype(jnp.int32)[None]
    ready = {}
    for u in reversed(upper):
        other = swap(new[sectors - 1 - u], "section")
        ready[u] = ready_step(flag, other, vecs[u])

    where = jnp.stack([section, me]).astype(jnp.int32)
    done = {}
    for u in reversed(upper):
        keep, send = apply_step(where, new[u], ready[u], peers)
        keep = keep + swap(send, "channel", 0).astype(F32)
        for bit in range(1, bits):
            pairs = keep.reshape((keep.shape[0] // 2, 2) + keep.shape[1:])
            keep = pairs[:, 0] + swap(pairs[:, 1].astype(BF16), "channel", bit).astype(F32)
        done[u] = (keep[0, 0].astype(BF16), swap(keep[0, 1].astype(BF16), "section"))

    blocks_q = [done[last - i][1] for i in range(sectors // 2)] + [done[u][0] for u in upper]
    ordered = jnp.stack(blocks_q, axis=1)
    new_psi = jnp.where(section == 0, ordered, jnp.flip(ordered, 1))[:, None]
    slots = jnp.stack([sector(u) for u in range(sectors)]).astype(jnp.int32)
    new_env = place_step(slots, [new[u] for u in range(sectors)])
    return (new_env[None], new_psi)


def is_pipelined(peers, chan, sectors, dim, states):
    return (
        peers > 1
        and peers & (peers - 1) == 0
        and sectors % 2 == 0
        and dim % 128 == 0
        and dim % (8 * peers) == 0
        and peers * chan * ROWS <= 512
        and states * chan * ROWS <= 512
    )


def per_device(env, site_tensor, mpo, channel_mask, block_mask, state_charge, psi):
    args = (env, site_tensor, mpo, channel_mask, block_mask, state_charge, psi)
    chan, sectors, dim = env.shape[1:4]
    peers = lax.axis_size("channel")
    if is_pipelined(peers, chan, sectors, dim, site_tensor.shape[1]):
        return pipelined_plan(*args)
    return general_plan(*args)


def solution(mesh):
    return jax.shard_map(
        per_device,
        mesh=mesh,
        in_specs=(
            P("section", "channel", "block", None, None),
            P("section", None, "block", None, None),
            P("section", None, None, None),
            P("section", None, None),
            P("section", None, "block"),
            P(),
            P("section", "block", None, None),
        ),
        out_specs=(
            P("section", "channel", "block", None, None),
            P("channel", "section", "block", None),
        ),
        check_vma=False,
    )
```

time: 683 us -> 388 us (0.57)
  waiting for transfers between devices: 460 us -> 222 us
  matrix products: 149 us -> 4.48 us
  Pallas kernels: 0 us -> 106 us
  local copies, waits for them, and re-layouts: 38.5 us -> 22.6 us
  starting transfers between devices: 7.6 us -> 21.6 us
  between operations: 14.1 us -> 0.92 us
    all_gather x1 -> x0, waiting for transfers between devices: 205 us -> none  [per_device(): gathered = lax.all_gather(own_env, 'channel', axis=0, tiled=True)]
    dot_general x5 -> x4, matrix products: 149 us -> 4.48 us  [mixer(): wide = spread_out @ table.astype(BF16) @ spread_in]
    pallas_call x0 -> x9, Pallas kernels: none -> 106 us  [the longest x4 72.4 us: sector_step(): pl.pallas_call(body, grid_spec=pltpu.PrefetchScalarGridSpec(num_scalar_pr...]
    reduce_scatter x1 -> x0, waiting for transfers between devices: 44.5 us -> none  [per_device(): lax.psum_scatter(jnp.einsum('wvqad,wqcd->avqc', applied, right_env, prefe...]
    dot_general x2 -> x0, local copies, waits for them, and re-layouts: 32.5 us -> none  [the longest x1 19.2 us: per_device(): jnp.einsum('vsqab,sq->vqab', contracted_layers, sector_present * (1.0 - c...]
    ppermute x3 -> x23, starting transfers between devices: 7.52 us -> 21.6 us  [the longest x22 16.4 us: swap(): lax.ppermute(value, axis, [(i, i ^ 1 << bit) for i in range(lax.axis_size...]
    unnamed x13 -> x26, local copies, waits for them, and re-layouts: 1.24 us -> 14.9 us
    ppermute x3 -> x23, waiting for transfers between devices: 209 us -> 222 us  [the longest x22 216 us: swap(): lax.ppermute(value, axis, [(i, i ^ 1 << bit) for i in range(lax.axis_size...]
  transfers between devices with their start and end apart: 5 -> 23, of which waited for: 5 -> 10; matrix products, arithmetic and copies ran while one was open for 3% -> 8% of each run, Pallas kernels for 0% -> 27%
where the time goes in v1:
time: 388 us; the launch traced here: 387 us
  waiting for transfers between devices  222 us (57%)
  Pallas kernels  106 us (27%)
  local copies, waits for them, and re-layouts  22.6 us (6%)
  starting transfers between devices  21.6 us (6%)
  other arithmetic  10.2 us (3%)
  matrix products  4.48 us (1%)
    ppermute x22, waiting for transfers between devices, swap(): lax.ppermute(value, axis, [(i, i ^ 1 << bit) for i in range(lax.axis_size...  216 us
    pallas_call x4, Pallas kernels, sector_step(): pl.pallas_call(body, grid_spec=pltpu.PrefetchScalarGridSpec(num_scalar_pr...  72.4 us
    ppermute x22, starting transfers between devices, swap(): lax.ppermute(value, axis, [(i, i ^ 1 << bit) for i in range(lax.axis_size...  16.4 us
    unnamed x26, local copies, waits for them, and re-layouts  14.9 us
    pallas_call x2, Pallas kernels, apply_step(): pl.pallas_call(apply_body, grid_spec=pltpu.PrefetchScalarGridSpec(num_sca...  13.2 us
    pallas_call x2, Pallas kernels, ready_step(): pl.pallas_call(ready_body, grid_spec=pltpu.PrefetchScalarGridSpec(num_sca...  12.2 us
  transfers between devices with their start and end apart: 23, of which 10 were waited for; matrix products, arithmetic and copies ran while one was open for 8% of the time, Pallas kernels for 27%

profile of v1, /device:TPU:0, one launch (start us, length us, event | category | flops | bytes accessed | tf_op | source)
XLA Modules:
  0.0 387.0 jit_solution(8403013781077973388)
XLA Ops:
  0.7 6.2 %dynamic-slice_bitcast_fusion = (bf16[4,512,512]{2,1,0:T(8,128)(2,1)}, bf16[4,512,512]{2,1,0:T(8,128)(2,1)}, bf16[4,512,512]{2,1,0:T(8,128)(2,1)}, bf16[4,512,512]{2,1,0:T(8,128)(2,1)S(1)}) fusion(bf16[1,4,4,512,512]{4,3,2,1,0:T(8,128)(2,1)} %param.7, s32[]{:T(128)} %select_n.159, s32[]{:T(128)} %select_n.160, s32[]{:T(128)} %select_n.157, s32[]{:T(128)} %select_n.158), kind=kLoop, calls=%fused_computation.1 | loop fusion | bytes 16777232 | tf_op jit(solution)/shard_map/jit(dynamic_index_in_dim)/squeeze | solution.py:281
  6.9 3.0 collective-permute-start.4
  12.5 44.2 %collective-permute-done.4.refs_2_ = bf16[4,512,512]{2,1,0:T(8,128)(2,1)} collective-permute-done((bf16[4,512,512]{2,1,0:T(8,128)(2,1)}, bf16[4,512,512]{2,1,0:T(8,128)(2,1)}, u32[]{:S(2)}, u32[]{:S(2)}) %collective-permute-start.4) | collective-permute-done | bytes 2097184 | tf_op jit(solution)/shard_map/ppermute | solution.py:277
  57.7 13.2 %copy.38 = bf16[1,4,4,512,512]{3,4,2,1,0:T(8,128)(2,1)} copy(bf16[1,4,4,512,512]{4,3,2,1,0:T(8,128)(2,1)} %param.8) | data formatting | bytes 16777216 | tf_op args[1]
  71.2 30.4 %collective-permute-done.1.refs_2_ = bf16[4,512,512]{2,1,0:T(8,128)(2,1)} collective-permute-done((bf16[4,512,512]{2,1,0:T(8,128)(2,1)}, bf16[4,512,512]{2,1,0:T(8,128)(2,1)}, u32[]{:S(2)}, u32[]{:S(2)}) %collective-permute-start.1) | collective-permute-done | bytes 2097184 | tf_op jit(solution)/shard_map/ppermute | solution.py:277
  107.1 39.4 %collective-permute-done.8.refs_2_ = bf16[4,512,512]{2,1,0:T(8,128)(2,1)} collective-permute-done((bf16[4,512,512]{2,1,0:T(8,128)(2,1)S(1)}, bf16[4,512,512]{2,1,0:T(8,128)(2,1)}, u32[]{:S(2)}, u32[]{:S(2)}) %collective-permute-start.8) | collective-permute-done | bytes 2097184 | tf_op jit(solution)/shard_map/ppermute | solution.py:277
  147.7 17.8 %shard_map.87 = (f32[4,512,512]{2,1,0:T(8,128)}, bf16[4,512,512]{2,1,0:T(8,128)(2,1)}) custom-call(s32[5]{0:T(128)} %get-tuple-element.63.sc, bf16[4,512,512]{2,1,0:T(8,128)(2,1)} %get-tuple-element.43.refs_0_, bf16[4,512,512]{2,1,0:T(8,128)(2,1)} %collective-permute-done.3.refs_1_, bf16[4,512,512]{2,1,0:T(8,128)(2,1)} %collective-permute-done.4.refs_2_, ...), custom_call_target="tpu_custom_call" | custom-call | flops 10737418240 | bytes 20971520 | tf_op jit(solution)/shard_map/pallas_call | solution.py:145
  165.7 25.0 %collective-permute-done.11.refs_2_ = bf16[4,512,512]{2,1,0:T(8,128)(2,1)} collective-permute-done((bf16[4,512,512]{2,1,0:T(8,128)(2,1)}, bf16[4,512,512]{2,1,0:T(8,128)(2,1)}, u32[]{:S(2)}, u32[]{:S(2)}) %collective-permute-start.11) | collective-permute-done | bytes 2097184 | tf_op jit(solution)/shard_map/ppermute | solution.py:277
  190.7 5.1 %collective-permute-start.6 = (bf16[4,512,512]{2,1,0:T(8,128)(2,1)}, bf16[4,512,512]{2,1,0:T(8,128)(2,1)}, u32[]{:S(2)}, u32[]{:S(2)}) collective-permute-start(bf16[4,512,512]{2,1,0:T(8,128)(2,1)} %get-tuple-element.15), channel_id=1, source_target_pairs={{0,1},{1,2},{2,3},{17,16},{18,17},{19,18},{4,5},{5,6},{6,7},{21,20... | collective-permute-start | bytes 6291464 | tf_op jit(solution)/shard_map/ppermute | solution.py:360
  195.8 17.8 %shard_map.86 = (f32[4,512,512]{2,1,0:T(8,128)}, bf16[4,512,512]{2,1,0:T(8,128)(2,1)}) custom-call(s32[5]{0:T(128)} %get-tuple-element.65.sc, bf16[4,512,512]{2,1,0:T(8,128)(2,1)} %get-tuple-element.44.refs_0_, bf16[4,512,512]{2,1,0:T(8,128)(2,1)} %collective-permute-done.refs_1_, bf16[4,512,512]{2,1,0:T(8,128)(2,1)} %collective-permute-done.1.refs_2_, ...), custom_call_target="tpu_custom_call" | custom-call | flops 10737418240 | bytes 20971520 | tf_op jit(solution)/shard_map/pallas_call | solution.py:145
  213.6 18.1 %shard_map.88 = (bf16[4,512,512]{2,1,0:T(8,128)(2,1)}, bf16[4,512,512]{2,1,0:T(8,128)(2,1)}) custom-call(s32[5]{0:T(128)} %get-tuple-element.64.sc, bf16[4,512,512]{2,1,0:T(8,128)(2,1)} %copy-done.2, bf16[4,512,512]{2,1,0:T(8,128)(2,1)} %collective-permute-done.7.refs_1_, bf16[4,512,512]{2,1,0:T(8,128)(2,1)} %collective-permute-done.8.refs_2_, ...), custom_call_target="tpu_custom_call" | custom-call | flops 10737418240 | bytes 20971520 | tf_op jit(solution)/shard_map/pallas_call | solution.py:145
  235.0 5.3 %collective-permute-done.6 = bf16[4,512,512]{2,1,0:T(8,128)(2,1)} collective-permute-done((bf16[4,512,512]{2,1,0:T(8,128)(2,1)}, bf16[4,512,512]{2,1,0:T(8,128)(2,1)}, u32[]{:S(2)}, u32[]{:S(2)}) %collective-permute-start.6) | collective-permute-done | bytes 2097184 | tf_op jit(solution)/shard_map/ppermute | solution.py:360
  240.3 2.5 add_convert_fusion.refs_0_
  242.7 2.5 collective-permute-start.13
  246.9 44.9 %collective-permute-done.19 = bf16[512,512]{1,0:T(8,128)(2,1)} collective-permute-done((bf16[512,512]{1,0:T(8,128)(2,1)}, bf16[512,512]{1,0:T(8,128)(2,1)}, u32[]{:S(2)}, u32[]{:S(2)}) %collective-permute-start.19) | collective-permute-done | bytes 524320 | tf_op jit(solution)/shard_map/ppermute | solution.py:277
  294.1 18.7 %shard_map.89 = (bf16[4,512,512]{2,1,0:T(8,128)(2,1)}, bf16[4,512,512]{2,1,0:T(8,128)(2,1)}) custom-call(s32[5]{0:T(128)} %get-tuple-element.62.sc, bf16[4,512,512]{2,1,0:T(8,128)(2,1)} %get-tuple-element.42.refs_0_, bf16[4,512,512]{2,1,0:T(8,128)(2,1)} %collective-permute-done.10.refs_1_, bf16[4,512,512]{2,1,0:T(8,128)(2,1)} %collective-permute-done.11.refs_2_, ...), custom_call_target="tpu_custom_call" | custom-call | flops 10737418240 | bytes 20971520 | tf_op jit(solution)/shard_map/pallas_call | solution.py:145
  312.8 6.1 %shard_map.93.ready = bf16[2,4,512,512]{3,2,1,0:T(8,128)(2,1)} custom-call(s32[1]{0:T(128)} %bitcast.31.sc, bf16[4,512,512]{2,1,0:T(8,128)(2,1)} %collective-permute-done.18.other, bf16[2,512,512]{2,1,0:T(8,128)(2,1)} %pad_maximum_fusion.1.vecs), custom_call_target="tpu_custom_call" | custom-call | flops 2147483648 | bytes 6291456 | tf_op jit(solution)/shard_map/pallas_call | solution.py:183
  318.9 6.4 %shard_map.94 = (f32[2,2,128,512]{3,2,1,0:T(8,128)}, bf16[2,2,128,512]{3,2,1,0:T(8,128)(2,1)}) custom-call(s32[2]{0:T(128)} %pad_add_fusion.5.sc, bf16[4,512,512]{2,1,0:T(8,128)(2,1)} %get-tuple-element.20.refs_2_.own, bf16[2,4,512,512]{3,2,1,0:T(8,128)(2,1)} %shard_map.93.ready), custom_call_target="tpu_custom_call" | custom-call | flops 2147483648 | bytes 6291456 | tf_op jit(solution)/shard_map/pallas_call | solution.py:235
  325.4 21.9 %collective-permute-done.14 = bf16[512,512]{1,0:T(8,128)(2,1)} collective-permute-done((bf16[512,512]{1,0:T(8,128)(2,1)}, bf16[512,512]{1,0:T(8,128)(2,1)}, u32[]{:S(2)}, u32[]{:S(2)}) %collective-permute-start.14) | collective-permute-done | bytes 524320 | tf_op jit(solution)/shard_map/ppermute | solution.py:277
  349.4 6.1 %shard_map.91.ready = bf16[2,4,512,512]{3,2,1,0:T(8,128)(2,1)} custom-call(s32[1]{0:T(128)} %bitcast.31.sc, bf16[4,512,512]{2,1,0:T(8,128)(2,1)} %collective-permute-done.13.other, bf16[2,512,512]{2,1,0:T(8,128)(2,1)} %pad_maximum_fusion.vecs), custom_call_target="tpu_custom_call" | custom-call | flops 2147483648 | bytes 6291456 | tf_op jit(solution)/shard_map/pallas_call | solution.py:183
  355.5 6.8 %shard_map.92 = (f32[2,2,128,512]{3,2,1,0:T(8,128)}, bf16[2,2,128,512]{3,2,1,0:T(8,128)(2,1)}) custom-call(s32[2]{0:T(128)} %pad_add_fusion.5.sc, bf16[4,512,512]{2,1,0:T(8,128)(2,1)} %get-tuple-element.21.refs_3_.own, bf16[2,4,512,512]{3,2,1,0:T(8,128)(2,1)} %shard_map.91.ready), custom_call_target="tpu_custom_call" | custom-call | flops 2147483648 | bytes 6291456 | tf_op jit(solution)/shard_map/pallas_call | solution.py:235
  366.2 5.6 %collective-permute-done.21 = bf16[1,2,128,512]{3,2,1,0:T(8,128)(2,1)S(1)} collective-permute-done((bf16[1,2,128,512]{3,2,1,0:T(8,128)(2,1)S(1)}, bf16[1,2,128,512]{3,2,1,0:T(8,128)(2,1)S(1)}, u32[]{:S(2)}, u32[]{:S(2)}) %collective-permute-start.21) | collective-permute-done | bytes 262176 | tf_op jit(solution)/shard_map/ppermute | solution.py:277
  372.2 4.7 %collective-permute-done.16 = bf16[1,2,128,512]{3,2,1,0:T(8,128)(2,1)S(1)} collective-permute-done((bf16[1,2,128,512]{3,2,1,0:T(8,128)(2,1)S(1)}, bf16[1,2,128,512]{3,2,1,0:T(8,128)(2,1)S(1)}, u32[]{:S(2)}, u32[]{:S(2)}) %collective-permute-start.16) | collective-permute-done | bytes 262176 | tf_op jit(solution)/shard_map/ppermute | solution.py:277
  377.9 7.6 %shard_map.90 = bf16[4,4,512,512]{3,2,1,0:T(8,128)(2,1)} custom-call(s32[4]{0:T(128)} %pad_add_fusion.sc, bf16[4,512,512]{2,1,0:T(8,128)(2,1)} %copy-done, bf16[4,512,512]{2,1,0:T(8,128)(2,1)} %get-tuple-element.17.refs_1_, bf16[4,512,512]{2,1,0:T(8,128)(2,1)} %get-tuple-element.20.refs_2_.own, bf16[4,512,512]{2,1,0:T(8,128)(2,1)} %get-tuple-element.21.refs_3_.own), custom_call_target="tpu_custom_call" | custom-call | tf_op jit(solution)/shard_map/pallas_call | solution.py:263
  (97 shorter events, 26.6 us)
Async XLA Ops:
  6.9 139.6 %copy-start.2 = (bf16[4,512,512]{2,1,0:T(8,128)(2,1)}, bf16[4,512,512]{2,1,0:T(8,128)(2,1)S(1)}, u32[]{:S(2)}) copy-start(bf16[4,512,512]{2,1,0:T(8,128)(2,1)S(1)} %get-tuple-element.45.refs_0_) | copy-start | bytes 6291460
  6.9 49.8 %collective-permute-start.4 = (bf16[4,512,512]{2,1,0:T(8,128)(2,1)}, bf16[4,512,512]{2,1,0:T(8,128)(2,1)}, u32[]{:S(2)}, u32[]{:S(2)}) collective-permute-start(bf16[4,512,512]{2,1,0:T(8,128)(2,1)} %get-tuple-element.43.refs_0_), channel_id=1, source_target_pairs={{0,8},{4,12},{8,0},{12,4},{1,9},{5,13},{9,1},{13,5},{2,10},{6,14},... | collective-permute-start | bytes 6291464 | tf_op jit(solution)/shard_map/ppermute | solution.py:277
  9.9 91.7 %collective-permute-start.1 = (bf16[4,512,512]{2,1,0:T(8,128)(2,1)}, bf16[4,512,512]{2,1,0:T(8,128)(2,1)}, u32[]{:S(2)}, u32[]{:S(2)}) collective-permute-start(bf16[4,512,512]{2,1,0:T(8,128)(2,1)} %get-tuple-element.44.refs_0_), channel_id=1, source_target_pairs={{0,8},{4,12},{8,0},{12,4},{1,9},{5,13},{9,1},{13,5},{2,10},{6,14},... | collective-permute-start | bytes 6291464 | tf_op jit(solution)/shard_map/ppermute | solution.py:277
  9.9 93.7 %collective-permute-start.3 = (bf16[4,512,512]{2,1,0:T(8,128)(2,1)}, bf16[4,512,512]{2,1,0:T(8,128)(2,1)}, u32[]{:S(2)}, u32[]{:S(2)}) collective-permute-start(bf16[4,512,512]{2,1,0:T(8,128)(2,1)} %get-tuple-element.43.refs_0_), channel_id=1, source_target_pairs={{0,4},{4,0},{8,12},{12,8},{1,5},{5,1},{9,13},{13,9},{2,6},{6,2},{1... | collective-permute-start | bytes 6291464 | tf_op jit(solution)/shard_map/ppermute | solution.py:277
  9.9 155.6 %collective-permute-start = (bf16[4,512,512]{2,1,0:T(8,128)(2,1)}, bf16[4,512,512]{2,1,0:T(8,128)(2,1)}, u32[]{:S(2)}, u32[]{:S(2)}) collective-permute-start(bf16[4,512,512]{2,1,0:T(8,128)(2,1)} %get-tuple-element.44.refs_0_), channel_id=1, source_target_pairs={{0,4},{4,0},{8,12},{12,8},{1,5},{5,1},{9,13},{13,9},{2,6},{6,2},{1... | collective-permute-start | bytes 6291464 | tf_op jit(solution)/shard_map/ppermute | solution.py:277
  10.4 136.1 %collective-permute-start.8 = (bf16[4,512,512]{2,1,0:T(8,128)(2,1)S(1)}, bf16[4,512,512]{2,1,0:T(8,128)(2,1)}, u32[]{:S(2)}, u32[]{:S(2)}) collective-permute-start(bf16[4,512,512]{2,1,0:T(8,128)(2,1)S(1)} %get-tuple-element.45.refs_0_), channel_id=1, source_target_pairs={{0,8},{4,12},{8,0},{12,4},{1,9},{5,13},{9,1},{13,5},{2,10},{6,14},... | collective-permute-start | bytes 6291464 | tf_op jit(solution)/shard_map/ppermute | solution.py:277
  56.7 89.9 %collective-permute-start.5 = (bf16[4,512,512]{2,1,0:T(8,128)(2,1)}, bf16[4,512,512]{2,1,0:T(8,128)(2,1)}, u32[]{:S(2)}, u32[]{:S(2)}) collective-permute-start(bf16[4,512,512]{2,1,0:T(8,128)(2,1)} %collective-permute-done.4.refs_2_), channel_id=1, source_target_pairs={{0,4},{4,0},{8,12},{12,8},{1,5},{5,1},{9,13},{13,9},{2,6},{6,2},{1... | collective-permute-start | bytes 6291464 | tf_op jit(solution)/shard_map/ppermute | solution.py:277
  101.6 89.0 %collective-permute-start.11 = (bf16[4,512,512]{2,1,0:T(8,128)(2,1)}, bf16[4,512,512]{2,1,0:T(8,128)(2,1)}, u32[]{:S(2)}, u32[]{:S(2)}) collective-permute-start(bf16[4,512,512]{2,1,0:T(8,128)(2,1)} %get-tuple-element.42.refs_0_), channel_id=1, source_target_pairs={{0,8},{4,12},{8,0},{12,4},{1,9},{5,13},{9,1},{13,5},{2,10},{6,14},... | collective-permute-start | bytes 6291464 | tf_op jit(solution)/shard_map/ppermute | solution.py:277
  103.7 87.0 %collective-permute-start.2 = (bf16[4,512,512]{2,1,0:T(8,128)(2,1)}, bf16[4,512,512]{2,1,0:T(8,128)(2,1)}, u32[]{:S(2)}, u32[]{:S(2)}) collective-permute-start(bf16[4,512,512]{2,1,0:T(8,128)(2,1)} %collective-permute-done.1.refs_2_), channel_id=1, source_target_pairs={{0,4},{4,0},{8,12},{12,8},{1,5},{5,1},{9,13},{13,9},{2,6},{6,2},{1... | collective-permute-start | bytes 6291464 | tf_op jit(solution)/shard_map/ppermute | solution.py:277
  146.6 67.0 %collective-permute-start.7 = (bf16[4,512,512]{2,1,0:T(8,128)(2,1)S(1)}, bf16[4,512,512]{2,1,0:T(8,128)(2,1)}, u32[]{:S(2)}, u32[]{:S(2)}) collective-permute-start(bf16[4,512,512]{2,1,0:T(8,128)(2,1)S(1)} %get-tuple-element.45.refs_0_), channel_id=1, source_target_pairs={{0,4},{4,0},{8,12},{12,8},{1,5},{5,1},{9,13},{13,9},{2,6},{6,2},{1... | collective-permute-start | bytes 6291464 | tf_op jit(solution)/shard_map/ppermute | solution.py:277
  146.6 67.0 %collective-permute-start.9 = (bf16[4,512,512]{2,1,0:T(8,128)(2,1)}, bf16[4,512,512]{2,1,0:T(8,128)(2,1)}, u32[]{:S(2)}, u32[]{:S(2)}) collective-permute-start(bf16[4,512,512]{2,1,0:T(8,128)(2,1)} %collective-permute-done.8.refs_2_), channel_id=1, source_target_pairs={{0,4},{4,0},{8,12},{12,8},{1,5},{5,1},{9,13},{13,9},{2,6},{6,2},{1... | collective-permute-start | bytes 6291464 | tf_op jit(solution)/shard_map/ppermute | solution.py:277
  165.5 128.5 %collective-permute-start.10 = (bf16[4,512,512]{2,1,0:T(8,128)(2,1)}, bf16[4,512,512]{2,1,0:T(8,128)(2,1)}, u32[]{:S(2)}, u32[]{:S(2)}) collective-permute-start(bf16[4,512,512]{2,1,0:T(8,128)(2,1)} %get-tuple-element.42.refs_0_), channel_id=1, source_target_pairs={{0,4},{4,0},{8,12},{12,8},{1,5},{5,1},{9,13},{13,9},{2,6},{6,2},{1... | collective-permute-start | bytes 6291464 | tf_op jit(solution)/shard_map/ppermute | solution.py:277
  190.7 103.4 %collective-permute-start.12 = (bf16[4,512,512]{2,1,0:T(8,128)(2,1)}, bf16[4,512,512]{2,1,0:T(8,128)(2,1)}, u32[]{:S(2)}, u32[]{:S(2)}) collective-permute-start(bf16[4,512,512]{2,1,0:T(8,128)(2,1)} %collective-permute-done.11.refs_2_), channel_id=1, source_target_pairs={{0,4},{4,0},{8,12},{12,8},{1,5},{5,1},{9,13},{13,9},{2,6},{6,2},{1... | collective-permute-start | bytes 6291464 | tf_op jit(solution)/shard_map/ppermute | solution.py:277
  190.7 49.6 %collective-permute-start.6 = (bf16[4,512,512]{2,1,0:T(8,128)(2,1)}, bf16[4,512,512]{2,1,0:T(8,128)(2,1)}, u32[]{:S(2)}, u32[]{:S(2)}) collective-permute-start(bf16[4,512,512]{2,1,0:T(8,128)(2,1)} %get-tuple-element.15), channel_id=1, source_target_pairs={{0,1},{1,2},{2,3},{17,16},{18,17},{19,18},{4,5},{5,6},{6,7},{21,20... | collective-permute-start | bytes 6291464 | tf_op jit(solution)/shard_map/ppermute | solution.py:360
  231.7 81.0 %collective-permute-start.18 = (bf16[4,512,512]{2,1,0:T(8,128)(2,1)}, bf16[4,512,512]{2,1,0:T(8,128)(2,1)}, u32[]{:S(2)}, u32[]{:S(2)}) collective-permute-start(bf16[4,512,512]{2,1,0:T(8,128)(2,1)} %get-tuple-element.17.refs_1_), channel_id=1, source_target_pairs={{0,16},{16,0},{1,17},{17,1},{2,18},{18,2},{3,19},{19,3},{4,20},{20... | collective-permute-start | bytes 6291464 | tf_op jit(solution)/shard_map/ppermute | solution.py:277
  233.0 58.9 %collective-permute-start.19 = (bf16[512,512]{1,0:T(8,128)(2,1)}, bf16[512,512]{1,0:T(8,128)(2,1)}, u32[]{:S(2)}, u32[]{:S(2)}) collective-permute-start(bf16[512,512]{1,0:T(8,128)(2,1)} %get-tuple-element.49), channel_id=1, source_target_pairs={{0,16},{16,0},{1,17},{17,1},{2,18},{18,2},{3,19},{19,3},{4,20},{20... | collective-permute-start | bytes 1572872 | tf_op jit(solution)/shard_map/ppermute | solution.py:277
  242.7 106.7 %collective-permute-start.13 = (bf16[4,512,512]{2,1,0:T(8,128)(2,1)S(1)}, bf16[4,512,512]{2,1,0:T(8,128)(2,1)}, u32[]{:S(2)}, u32[]{:S(2)}) collective-permute-start(bf16[4,512,512]{2,1,0:T(8,128)(2,1)S(1)} %add_convert_fusion.refs_0_), channel_id=1, source_target_pairs={{0,16},{16,0},{1,17},{17,1},{2,18},{18,2},{3,19},{19,3},{4,20},{20... | collective-permute-start | bytes 6291464 | tf_op jit(solution)/shard_map/ppermute | solution.py:277
  291.9 55.4 %collective-permute-start.14 = (bf16[512,512]{1,0:T(8,128)(2,1)}, bf16[512,512]{1,0:T(8,128)(2,1)}, u32[]{:S(2)}, u32[]{:S(2)}) collective-permute-start(bf16[512,512]{1,0:T(8,128)(2,1)} %get-tuple-element.47), channel_id=1, source_target_pairs={{0,16},{16,0},{1,17},{17,1},{2,18},{18,2},{3,19},{19,3},{4,20},{20... | collective-permute-start | bytes 1572872 | tf_op jit(solution)/shard_map/ppermute | solution.py:277
  325.4 37.0 %collective-permute-start.20 = (bf16[2,2,128,512]{3,2,1,0:T(8,128)(2,1)}, bf16[2,2,128,512]{3,2,1,0:T(8,128)(2,1)S(1)}, u32[]{:S(2)}, u32[]{:S(2)}) collective-permute-start(bf16[2,2,128,512]{3,2,1,0:T(8,128)(2,1)} %get-tuple-element.25), channel_id=1, source_target_pairs={{0,4},{4,0},{8,12},{12,8},{1,5},{5,1},{9,13},{13,9},{2,6},{6,2},{1... | collective-permute-start | bytes 1572872 | tf_op jit(solution)/shard_map/ppermute | solution.py:277
  362.3 2.1 collective-permute-start.15
  362.6 9.2 %collective-permute-start.21 = (bf16[1,2,128,512]{3,2,1,0:T(8,128)(2,1)S(1)}, bf16[1,2,128,512]{3,2,1,0:T(8,128)(2,1)S(1)}, u32[]{:S(2)}, u32[]{:S(2)}) collective-permute-start(bf16[1,2,128,512]{3,2,1,0:T(8,128)(2,1)S(1)} %fusion.14), channel_id=1, source_target_pairs={{0,8},{4,12},{8,0},{12,4},{1,9},{5,13},{9,1},{13,5},{2,10},{6,14},... | collective-permute-start | bytes 786440 | tf_op jit(solution)/shard_map/ppermute | solution.py:277
  364.7 12.3 %collective-permute-start.16 = (bf16[1,2,128,512]{3,2,1,0:T(8,128)(2,1)S(1)}, bf16[1,2,128,512]{3,2,1,0:T(8,128)(2,1)S(1)}, u32[]{:S(2)}, u32[]{:S(2)}) collective-permute-start(bf16[1,2,128,512]{3,2,1,0:T(8,128)(2,1)S(1)} %fusion.13), channel_id=1, source_target_pairs={{0,8},{4,12},{8,0},{12,4},{1,9},{5,13},{9,1},{13,5},{2,10},{6,14},... | collective-permute-start | bytes 786440 | tf_op jit(solution)/shard_map/ppermute | solution.py:277
  371.9 13.7 %collective-permute-start.22 = (bf16[128,512]{1,0:T(8,128)(2,1)S(1)}, bf16[128,512]{1,0:T(8,128)(2,1)S(1)}, u32[]{:S(2)}, u32[]{:S(2)}) collective-permute-start(bf16[128,512]{1,0:T(8,128)(2,1)S(1)} %get-tuple-element.52), channel_id=1, source_target_pairs={{0,16},{16,0},{1,17},{17,1},{2,18},{18,2},{3,19},{19,3},{4,20},{20... | collective-permute-start | bytes 393224 | tf_op jit(solution)/shard_map/ppermute | solution.py:277
  377.1 8.5 %collective-permute-start.17 = (bf16[128,512]{1,0:T(8,128)(2,1)S(1)}, bf16[128,512]{1,0:T(8,128)(2,1)S(1)}, u32[]{:S(2)}, u32[]{:S(2)}) collective-permute-start(bf16[128,512]{1,0:T(8,128)(2,1)S(1)} %get-tuple-element.50), channel_id=1, source_target_pairs={{0,16},{16,0},{1,17},{17,1},{2,18},{18,2},{3,19},{19,3},{4,20},{20... | collective-permute-start | bytes 393224 | tf_op jit(solution)/shard_map/ppermute | solution.py:277
  (9 other events, 243.4 us)

commit v2 on v0

v2 whole, which is shorter than its diff:
```python
import functools

import jax
import jax.numpy as jnp
from jax import lax
from jax.experimental import pallas as pl
from jax.experimental.pallas import tpu as pltpu
from jax.sharding import PartitionSpec as P


ROWS = 16
F32 = jnp.float32
BF16 = jnp.bfloat16


def padded(block, sides, width):
    for axis, dim in sides:
        count = lax.axis_size(axis)
        forward = [(i, i + 1) for i in range(count - 1)]
        backward = [(target, source) for source, target in forward]
        low = lax.ppermute(
            lax.slice_in_dim(block, block.shape[dim] - width, None, axis=dim), axis, forward
        )
        high = lax.ppermute(lax.slice_in_dim(block, 0, width, axis=dim), axis, backward)
        block = jnp.concatenate([low, block, high], axis=dim)
    return block


def from_partner(value, axis, bit):
    return lax.ppermute(value, axis, [(i, i ^ 1 << bit) for i in range(lax.axis_size(axis))])


def general_plan(env, site_tensor, mpo, channel_mask, block_mask, state_charge, psi):
    section = lax.axis_index("section")
    own_env = env[0]
    site_blocks = site_tensor[0]
    weights = mpo[0] * channel_mask[0].astype(BF16)[:, :, None]
    chan_dev = own_env.shape[0]
    offset_w = lax.axis_index("channel") * chan_dev
    gathered = lax.all_gather(own_env, "channel", axis=0, tiled=True)
    local_w = lax.dynamic_slice_in_dim(weights, offset_w, chan_dev, 1)
    blended = jnp.einsum(
        "wvs,wqab->vsqab", local_w, gathered, preferred_element_type=F32
    ).astype(BF16)
    product = jnp.einsum(
        "vsqac,sqcb->vsqab", blended, site_blocks, preferred_element_type=F32
    ).astype(BF16)
    layers = jnp.einsum("sqca,vsqcb->vsqab", site_blocks, product, preferred_element_type=F32)
    charge_label = state_charge.astype(F32)
    present = block_mask[0].astype(F32)
    resident = jnp.einsum("vsqab,sq->vqab", layers, present * (1.0 - charge_label)[:, None])
    outgoing = jnp.einsum("vsqab,sq->vqab", layers, present * charge_label[:, None]).astype(BF16)
    rim_cells = padded(outgoing, (("block", 1),), 1)
    sector_count = outgoing.shape[1]
    shifted = jnp.where(section == 0, rim_cells[:, :sector_count], rim_cells[:, 2:])
    new_env = (resident + shifted.astype(F32)).astype(BF16)
    partner = from_partner(new_env, "section", 0)
    left_env = jnp.where(section == 0, new_env, partner)
    right_env = jnp.where(section == 0, partner, new_env)
    applied = jnp.einsum(
        "wqab,vqbd->wvqad", left_env, psi, preferred_element_type=F32
    ).astype(BF16)
    summed = lax.psum_scatter(
        jnp.einsum("wvqad,wqcd->avqc", applied, right_env, preferred_element_type=F32),
        "channel",
        scatter_dimension=0,
        tiled=True,
    )
    return (new_env[None], summed.astype(BF16))


def dot_nn(a, b):
    return lax.dot_general(a, b, (((1,), (0,)), ((), ())), preferred_element_type=F32)


def dot_nt(a, b):
    return lax.dot_general(a, b, (((1,), (1,)), ((), ())), preferred_element_type=F32)


VMEM = pl.BlockSpec(memory_space=pltpu.VMEM)
SMEM = pl.BlockSpec(memory_space=pltpu.SMEM)
HBM = pl.BlockSpec(memory_space=pltpu.HBM)


def in_hbm(array):
    return pltpu.with_memory_space_constraint(array, pltpu.HBM)


def pick_body(start, index, array, out, sem):
    rows = pl.ds(start, out.shape[1])
    copy = pltpu.make_async_copy(array.at[:, index[0], rows], out, sem)
    copy.start()
    copy.wait()


def pick_block(array, index, start, rows):
    lead, _, _, cols = array.shape
    return pl.pallas_call(
        functools.partial(pick_body, start),
        in_specs=[SMEM, HBM],
        out_specs=VMEM,
        out_shape=jax.ShapeDtypeStruct((lead, rows, cols), array.dtype),
        scratch_shapes=[pltpu.SemaphoreType.DMA],
        compiler_params=pltpu.CompilerParams(vmem_limit_bytes=4 << 20),
    )(index[None].astype(jnp.int32), in_hbm(array))


def turn_body(sc, site, plain, turned, blocks, flips, sems):
    count = blocks.shape[0]
    loads = [
        pltpu.make_async_copy(site.at[sc[1 + s], sc[0]], blocks.at[s], sems.at[0, s]) for s in range(count)
    ]
    for load in loads:
        load.start()
    stores = []
    for s in range(count):
        loads[s].wait()
        stores.append(pltpu.make_async_copy(blocks.at[s], plain.at[s], sems.at[1, s]))
        stores[-1].start()
        flips[s] = blocks[s].T
        stores.append(pltpu.make_async_copy(flips.at[s], turned.at[s], sems.at[2, s]))
        stores[-1].start()
    for store in stores:
        store.wait()


def turn_blocks(scalars, site):
    states, _, dim, _ = site.shape
    shape = pltpu.HBM((states, dim, dim), site.dtype)
    return pl.pallas_call(
        turn_body,
        in_specs=[SMEM, HBM],
        out_specs=[HBM, HBM],
        out_shape=[shape, shape],
        scratch_shapes=[
            pltpu.VMEM((states, dim, dim), site.dtype),
            pltpu.VMEM((states, dim, dim), site.dtype),
            pltpu.SemaphoreType.DMA((3, states)),
        ],
        compiler_params=pltpu.CompilerParams(vmem_limit_bytes=8 << 20),
    )(scalars, in_hbm(site))


def sector_body(plan, *refs):
    peers, groups_n, start, sides = plan
    refs = list(refs)
    groups = [[refs.pop(0) for _ in range(peers)] for _ in range(groups_n)]
    mixer, site, site_t = [refs.pop(0) for _ in range(3)]
    adds = [[refs.pop(0) if used else None for used in side[1:3]] for side in sides]
    outs = [refs.pop(0) for _ in sides]
    mixed, prod = refs
    chan, _, dim = groups[0][0].shape
    total = sum(group[0].shape[1] for group in groups)
    half = site.shape[0] // 2
    per_side = half * chan
    lead = sides[0][0] * per_side * ROWS
    weight = mixer[lead : lead + len(sides) * per_side * ROWS, :]

    def mix(pieces, strip, ahead, step, carry):
        first_row = pl.multiple_of(step * strip, strip)
        for group in range(strip // ROWS):
            at = pl.ds(first_row + group * ROWS, ROWS)
            slab = jnp.concatenate([p[:, at, :].reshape(chan * ROWS, dim) for p in pieces], axis=0)
            out = dot_nn(weight, slab).astype(BF16)
            mixed[:, pl.ds(group * ROWS, ROWS), :] = out.reshape(len(sides) * per_side, ROWS, dim)
        for n, (side, *_) in enumerate(sides):
            for k in range(half):
                first = n * per_side + k * chan
                left = mixed[first : first + chan, :strip].reshape(chan * strip, dim)
                out = dot_nn(left, site[side * half + k]).astype(BF16).reshape(chan, strip, dim)
                at = pl.ds(pl.multiple_of(k * total + ahead + first_row, 128), strip)
                prod[n * chan : (n + 1) * chan, at, :] = out
        return carry

    ahead = 0
    for pieces in groups:
        rows = pieces[0].shape[1]
        strip = strip_of(rows)
        lax.fori_loop(0, rows // strip, functools.partial(mix, pieces, strip, ahead), 0)
        ahead += rows

    def join(v, carry):
        for n, (side, _, _, wide) in enumerate(sides):
            left = [site_t[side * half + k, :, start : start + total] for k in range(half)]
            value = dot_nn(jnp.concatenate(left, axis=1), prod[n * chan + v])
            base, late = adds[n]
            if base is not None:
                value += base[v]
            if side == 1 and not wide:
                value = value.astype(BF16).astype(F32)
            if late is not None:
                value += late[v].astype(F32)
            outs[n][v] = value.astype(F32 if wide else BF16)
        return carry

    lax.fori_loop(0, chan, join, 0)


def strip_of(rows):
    return 256 if rows % 256 == 0 else 128


def sector_step(groups, mixer, site, site_t, start, sides):
    chan, _, dim = groups[0][0].shape
    rows = [group[0].shape[1] for group in groups]
    total = sum(rows)
    strip = max(strip_of(r) for r in rows)
    half = site.shape[0] // 2
    count = len(sides)
    peers = len(groups[0])
    extra = [x for side in sides for x in side[1:3] if x is not None]
    marks = tuple((side, base is not None, late is not None, wide) for side, base, late, wide in sides)
    return pl.pallas_call(
        functools.partial(sector_body, (peers, len(groups), start, marks)),
        in_specs=[VMEM] * (len(groups) * peers + 3 + len(extra)),
        out_specs=[VMEM] * count,
        out_shape=[jax.ShapeDtypeStruct((chan, dim, dim), F32 if side[3] else BF16) for side in sides],
        scratch_shapes=[
            pltpu.VMEM((count * half * chan, strip, dim), BF16),
            pltpu.VMEM((count * chan, half * total, dim), BF16),
        ],
        compiler_params=pltpu.CompilerParams(vmem_limit_bytes=STEP_LIMIT),
        cost_estimate=pl.CostEstimate(
            flops=4 * dim * dim * total * chan * half * count,
            transcendentals=0,
            bytes_accessed=2 * dim * total * chan * 8,
        ),
    )(*[piece for group in groups for piece in group], mixer, site, site_t, *extra)


STEP_LIMIT = 40 << 20


def ready_body(flag, other, mine, theirs, out):
    def each(w, carry):
        for n, vec in enumerate((mine, theirs)):

            @pl.when(flag[0] == 0)
            def _():
                out[n, w] = dot_nt(vec[...], other[w]).astype(BF16)

            @pl.when(flag[0] != 0)
            def _():
                out[n, w] = dot_nn(other[w], vec[...]).astype(BF16)

        return carry

    lax.fori_loop(0, other.shape[0], each, 0)


def ready_step(section, other, vecs):
    chan, dim, _ = other.shape
    return pl.pallas_call(
        ready_body,
        in_specs=[SMEM, VMEM, VMEM, VMEM],
        out_specs=VMEM,
        out_shape=jax.ShapeDtypeStruct((2, chan, dim, dim), BF16),
        compiler_params=pltpu.CompilerParams(vmem_limit_bytes=STEP_LIMIT),
        cost_estimate=pl.CostEstimate(
            flops=4 * dim**3 * chan, transcendentals=0, bytes_accessed=2 * dim * dim * chan * 3
        ),
    )(section, other, *vecs)


def apply_body(n, sc, own, ready, keep, send, acc):
    chan = own.shape[0]
    rows = keep.shape[-2]

    @pl.when(sc[0] == 0)
    def _():
        total = dot_nn(own[0], ready[n, 0])
        for w in range(1, chan):
            total += dot_nn(own[w], ready[n, w])
        acc[...] = total

    @pl.when(sc[0] != 0)
    def _():
        total = dot_nt(ready[n, 0], own[0])
        for w in range(1, chan):
            total += dot_nt(ready[n, w], own[w])
        acc[...] = total

    for j in range(2 * keep.shape[0]):
        start = pl.multiple_of((sc[1] ^ j) * rows, rows)
        value = acc[pl.ds(start, rows), :]
        if j % 2:
            send[j // 2] = value.astype(BF16)
        else:
            keep[j // 2] = value


def apply_step(n, scalars, own, ready, slots):
    chan, dim, _ = own.shape
    shape = (slots // 2, dim // slots, dim)
    return pl.pallas_call(
        functools.partial(apply_body, n),
        in_specs=[SMEM, VMEM, VMEM],
        out_specs=[VMEM, VMEM],
        out_shape=[jax.ShapeDtypeStruct(shape, F32), jax.ShapeDtypeStruct(shape, BF16)],
        scratch_shapes=[pltpu.VMEM((dim, dim), F32)],
        compiler_params=pltpu.CompilerParams(vmem_limit_bytes=STEP_LIMIT),
        cost_estimate=pl.CostEstimate(
            flops=2 * dim**3 * chan, transcendentals=0, bytes_accessed=2 * dim * dim * chan * 3
        ),
    )(scalars, own, ready)


def place_body(count, slots, *refs):
    out, sems = refs[-2:]
    copies = [
        pltpu.make_async_copy(refs[u], out.at[:, slots[u]], sems.at[u]) for u in range(count)
    ]
    for copy in copies:
        copy.start()
    for copy in copies:
        copy.wait()


def place_step(slots, parts, sectors, onto=None):
    chan, dim, _ = parts[0].shape
    count = len(parts)
    extra = [] if onto is None else [onto]
    return pl.pallas_call(
        functools.partial(place_body, count),
        in_specs=[SMEM] + [VMEM] * count + [HBM] * len(extra),
        out_specs=HBM,
        out_shape=jax.ShapeDtypeStruct((chan, sectors, dim, dim), parts[0].dtype),
        scratch_shapes=[pltpu.SemaphoreType.DMA((count,))],
        input_output_aliases={1 + count: 0} if extra else {},
        compiler_params=pltpu.CompilerParams(vmem_limit_bytes=4 << 20),
    )(slots, *parts, *extra)


def swap(value, axis, bit=0):
    return lax.ppermute(value, axis, [(i, i ^ (1 << bit)) for i in range(lax.axis_size(axis))])


def pick(array, index, axis):
    return lax.dynamic_index_in_dim(array, index, axis, keepdims=False)


def sector_order(sectors):
    return [sectors - 1] + list(range(sectors - 1))


def pipelined_plan(env, site_tensor, mpo, channel_mask, block_mask, state_charge, psi):
    section = lax.axis_index("section")
    me = lax.axis_index("channel")
    peers = lax.axis_size("channel")
    bits = peers.bit_length() - 1
    blocks = lax.axis_size("block")
    own_env = env[0]
    chan, sectors, dim, _ = own_env.shape
    site = site_tensor[0]
    states = site.shape[0]

    def sector(u):
        return jnp.where(section == 0, u, sectors - 1 - u)

    order = sector_order(sectors)

    def gather(u, start, rows):
        pieces = {0: pick_block(own_env, sector(u), start, rows)}
        for bit in reversed(range(bits)):
            moved = {}
            for j, p in pieces.items():
                moved[j | 1 << bit] = swap(p, "channel", bit)
            pieces.update(moved)
        return [pieces[j] for j in range(peers)]

    split = split_rows(dim)
    gathered = {}
    for u in order:
        if u in (order[0], order[-1]):
            gathered[u] = [gather(u, 0, split), gather(u, split, dim - split)]
        else:
            gathered[u] = [gather(u, 0, dim)]

    upper = range(sectors // 2, sectors)
    vecs = {}
    for u in upper:
        mine = pick(psi[0], sector(u), 0)
        theirs = swap(pick(psi[0], sector(sectors - 1 - u), 0), "section")
        vecs[u] = (mine, theirs)

    inputs = peers * chan
    outputs = states * chan
    key = state_charge * states + jnp.arange(states, dtype=jnp.int32)
    rank = jnp.sum((key[None, :] < key[:, None]).astype(jnp.int32), axis=1)
    chosen = rank[None, :] == jnp.arange(states, dtype=jnp.int32)[:, None]
    state_ids = jnp.arange(states, dtype=jnp.int32)[None, :]
    state_order = jnp.sum(jnp.where(chosen, state_ids, 0), axis=1)
    weights = mpo[0].astype(F32) * channel_mask[0].astype(F32)[:, :, None]
    weights = lax.dynamic_slice_in_dim(weights, me * chan, chan, 1)
    weights = weights.reshape(peers, chan, chan, states)
    weights = jnp.stack([pick(weights, me ^ j, 0) for j in range(peers)])
    weights = weights.reshape(inputs, chan, states)
    out_row = jnp.arange(outputs * ROWS)[:, None]
    in_row = jnp.arange(inputs * ROWS)[None, :]
    spread_out = (out_row // ROWS == jnp.arange(outputs)[None, :]).astype(BF16)
    spread_in = (in_row // ROWS == jnp.arange(inputs)[:, None]).astype(BF16)
    same_row = out_row % ROWS == in_row % ROWS

    def mixer(u):
        present = pick(block_mask[0], sector(u), 1).astype(F32)
        by_state = jnp.moveaxis(weights * present, 2, 0)
        picked = jnp.where(chosen[:, :, None, None], by_state[None], 0.0)
        table = jnp.swapaxes(jnp.sum(picked, axis=1), 1, 2).reshape(outputs, inputs)
        wide = spread_out @ table.astype(BF16) @ spread_in
        return jnp.where(same_row, wide, 0).astype(BF16)

    def scalars(u):
        return jnp.concatenate([sector(u)[None], state_order]).astype(jnp.int32)

    turned = {}
    for u in order:
        scalar = scalars(u)
        turned[u] = turn_blocks(scalar, site)

    def step(u, groups, start, *sides):
        return sector_step(groups, mixer(u), *turned[u], start, sides)

    links = [(b, b + 1) for b in range(blocks - 1)]
    links += [(blocks + b + 1, blocks + b) for b in range(blocks - 1)]

    new = {}
    last, end = order[0], order[-1]
    early, late = ([group] for group in gathered[last])
    [part] = step(last, early, 0, (1, None, None, True))
    [moving] = step(last, late, split, (1, part, None, False))
    raised = lax.ppermute(moving, ("section", "block"), links)
    [hold] = step(last, gathered[last], 0, (0, None, None, True))
    for u in order[1:-1]:
        if u == 0:
            [stay] = step(u, gathered[u], 0, (0, None, None, True))
            new[u] = (stay + raised.astype(F32)).astype(BF16)
            [moving] = step(u, gathered[u], 0, (1, None, None, False))
        else:
            new[u], moving = step(
                u, gathered[u], 0, (0, None, moving, False), (1, None, None, False)
            )
    early, late = ([group] for group in gathered[end])
    parts = step(end, early, 0, (0, None, None, True), (1, None, None, True))
    new[end], new[last] = step(
        end, late, split, (0, parts[0], moving, False), (1, parts[1], hold, False)
    )

    flag = section.astype(jnp.int32)[None]
    ready = {}
    for u in reversed(upper):
        other = swap(new[sectors - 1 - u], "section")
        ready[u] = ready_step(flag, other, vecs[u])

    where = jnp.stack([section, me]).astype(jnp.int32)
    done = {}
    for u in reversed(upper):
        ends = []
        for n in (1, 0):
            keep, send = apply_step(n, where, new[u], ready[u], peers)
            keep = keep + swap(send, "channel", 0).astype(F32)
            for bit in range(1, bits):
                pairs = keep.reshape((keep.shape[0] // 2, 2) + keep.shape[1:])
                keep = pairs[:, 0] + swap(pairs[:, 1].astype(BF16), "channel", bit).astype(F32)
            ends.append(keep[0].astype(BF16))
        done[u] = (ends[1], swap(ends[0], "section"))

    blocks_q = [done[last - i][1] for i in range(sectors // 2)] + [done[u][0] for u in upper]
    ordered = jnp.stack(blocks_q, axis=1)
    new_psi = jnp.where(section == 0, ordered, jnp.flip(ordered, 1))[:, None]
    new_env = None
    for us in (order[1:-1], [order[-1], order[0]]):
        slots = jnp.stack([sector(u) for u in us]).astype(jnp.int32)
        new_env = place_step(slots, [new[u] for u in us], sectors, new_env)
    return (new_env[None], new_psi)


def split_rows(dim):
    return dim // 4 * 3


def is_pipelined(peers, chan, sectors, dim, states):
    return (
        peers > 1
        and peers & (peers - 1) == 0
        and sectors % 2 == 0
        and sectors == 4
        and peers == 4
        and states % 2 == 0
        and dim % 512 == 0
        and dim % (8 * peers) == 0
        and peers * chan * ROWS <= 512
        and states * chan * ROWS <= 512
    )


def per_device(env, site_tensor, mpo, channel_mask, block_mask, state_charge, psi):
    args = (env, site_tensor, mpo, channel_mask, block_mask, state_charge, psi)
    chan, sectors, dim = env.shape[1:4]
    peers = lax.axis_size("channel")
    if is_pipelined(peers, chan, sectors, dim, site_tensor.shape[1]):
        return pipelined_plan(*args)
    return general_plan(*args)


def solution(mesh):
    return jax.shard_map(
        per_device,
        mesh=mesh,
        in_specs=(
            P("section", "channel", "block", None, None),
            P("section", None, "block", None, None),
            P("section", None, None, None),
            P("section", None, None),
            P("section", None, "block"),
            P(),
            P("section", "block", None, None),
        ),
        out_specs=(
            P("section", "channel", "block", None, None),
            P("channel", "section", "block", None),
        ),
        check_vma=False,
    )
```

time: 683 us -> 372 us (0.54)
  waiting for transfers between devices: 460 us -> 179 us
  matrix products: 149 us -> 1.86 us
  Pallas kernels: 0 us -> 136 us
  starting transfers between devices: 7.6 us -> 25.3 us
  local copies, waits for them, and re-layouts: 38.5 us -> 22 us
  between operations: 14.1 us -> 1.29 us
  other arithmetic: 12.8 us -> 5.49 us
    all_gather x1 -> x0, waiting for transfers between devices: 205 us -> none  [per_device(): gathered = lax.all_gather(own_env, 'channel', axis=0, tiled=True)]
    dot_general x5 -> x4, matrix products: 149 us -> 1.86 us  [mixer(): wide = spread_out @ table.astype(BF16) @ spread_in]
    pallas_call x0 -> x26, Pallas kernels: none -> 136 us  [the longest x8 87.2 us: sector_step(): pl.pallas_call(functools.partial(sector_body, (peers, len(groups), start,...]
    reduce_scatter x1 -> x0, waiting for transfers between devices: 44.5 us -> none  [per_device(): lax.psum_scatter(jnp.einsum('wvqad,wqcd->avqc', applied, right_env, prefe...]
    dot_general x2 -> x0, local copies, waits for them, and re-layouts: 32.5 us -> none  [the longest x1 19.2 us: per_device(): jnp.einsum('vsqab,sq->vqab', contracted_layers, sector_present * (1.0 - c...]
    ppermute x3 -> x33, waiting for transfers between devices: 209 us -> 179 us  [the longest x32 179 us: swap(): lax.ppermute(value, axis, [(i, i ^ 1 << bit) for i in range(lax.axis_size...]
    unnamed x13 -> x75, local copies, waits for them, and re-layouts: 1.24 us -> 20.3 us
    ppermute x3 -> x33, starting transfers between devices: 7.52 us -> 25.3 us  [the longest x32 20.2 us: swap(): lax.ppermute(value, axis, [(i, i ^ 1 << bit) for i in range(lax.axis_size...]
  transfers between devices with their start and end apart: 5 -> 33, of which waited for: 5 -> 10; matrix products, arithmetic and copies ran while one was open for 3% -> 3% of each run, Pallas kernels for 0% -> 36%
where the time goes in v2:
time: 372 us; the launch traced here: 371 us
  waiting for transfers between devices  179 us (48%)
  Pallas kernels  136 us (37%)
  starting transfers between devices  25.3 us (7%)
  local copies, waits for them, and re-layouts  22 us (6%)
  other arithmetic  5.49 us (1%)
    ppermute x32, waiting for transfers between devices, swap(): lax.ppermute(value, axis, [(i, i ^ 1 << bit) for i in range(lax.axis_size...  179 us
    pallas_call x8, Pallas kernels, sector_step(): pl.pallas_call(functools.partial(sector_body, (peers, len(groups), start,...  87.2 us
    unnamed x75, local copies, waits for them, and re-layouts  20.3 us
    ppermute x32, starting transfers between devices, swap(): lax.ppermute(value, axis, [(i, i ^ 1 << bit) for i in range(lax.axis_size...  20.2 us
    pallas_call x4, Pallas kernels, turn_blocks(): pl.pallas_call(turn_body, in_specs=[SMEM, HBM], out_specs=[HBM, HBM], out...  15.6 us
    pallas_call x6, Pallas kernels, pick_block(): pl.pallas_call(functools.partial(pick_body, start), in_specs=[SMEM, HBM],...  11.2 us
    pallas_call x2, Pallas kernels, ready_step(): pl.pallas_call(ready_body, in_specs=[SMEM, VMEM, VMEM, VMEM], out_specs=V...  9.36 us
  transfers between devices with their start and end apart: 33, of which 10 were waited for; matrix products, arithmetic and copies ran while one was open for 3% of the time, Pallas kernels for 36%

profile of v2, /device:TPU:0, one launch (start us, length us, event | category | flops | bytes accessed | tf_op | source)
XLA Modules:
  0.0 371.3 jit_solution(14126872650196225359)
XLA Ops:
  1.7 3.0 collective-permute-start.16
  11.3 6.3 %collective-permute-done.16.refs_6_.refs_2_ = bf16[4,128,512]{2,1,0:T(8,128)(2,1)} collective-permute-done((bf16[4,128,512]{2,1,0:T(8,128)(2,1)S(1)}, bf16[4,128,512]{2,1,0:T(8,128)(2,1)}, u32[]{:S(2)}, u32[]{:S(2)}) %collective-permute-start.16) | collective-permute-done | bytes 524320 | tf_op jit(solution)/shard_map/ppermute | solution.py:335
  27.3 68.9 %collective-permute-done.13.refs_2_ = bf16[4,384,512]{2,1,0:T(8,128)(2,1)} collective-permute-done((bf16[4,384,512]{2,1,0:T(8,128)(2,1)S(1)}, bf16[4,384,512]{2,1,0:T(8,128)(2,1)}, u32[]{:S(2)}, u32[]{:S(2)}) %collective-permute-start.13) | collective-permute-done | bytes 1572896 | tf_op jit(solution)/shard_map/ppermute | solution.py:335
  100.0 3.7 shard_map.98
  103.7 3.7 %shard_map.93 = (bf16[4,512,512]{2,1,0:T(8,128)(2,1)}, bf16[4,512,512]{2,1,0:T(8,128)(2,1)}) custom-call(s32[5]{0:T(128)S(1)} %get-tuple-element.76.sc, bf16[4,4,512,512]{3,2,1,0:T(8,128)(2,1)} %bitcast.115), custom_call_target="tpu_custom_call" | custom-call | tf_op jit(solution)/shard_map/pallas_call | solution.py:130
  107.5 3.9 %shard_map.91 = (bf16[4,512,512]{2,1,0:T(8,128)(2,1)}, bf16[4,512,512]{2,1,0:T(8,128)(2,1)}) custom-call(s32[5]{0:T(128)S(1)} %get-tuple-element.75.sc, bf16[4,4,512,512]{3,2,1,0:T(8,128)(2,1)} %bitcast.116), custom_call_target="tpu_custom_call" | custom-call | tf_op jit(solution)/shard_map/pallas_call | solution.py:130
  111.4 62.7 %collective-permute-done.4.refs_2_ = bf16[4,384,512]{2,1,0:T(8,128)(2,1)} collective-permute-done((bf16[4,384,512]{2,1,0:T(8,128)(2,1)}, bf16[4,384,512]{2,1,0:T(8,128)(2,1)}, u32[]{:S(2)}, u32[]{:S(2)}) %collective-permute-start.4) | collective-permute-done | bytes 1572896 | tf_op jit(solution)/shard_map/ppermute | solution.py:335
  183.0 9.5 %shard_map.102.refs_7_ = f32[4,512,512]{2,1,0:T(8,128)} custom-call(bf16[4,384,512]{2,1,0:T(8,128)(2,1)S(1)} %copy-done.5, bf16[4,384,512]{2,1,0:T(8,128)(2,1)S(1)} %copy-done.8, bf16[4,384,512]{2,1,0:T(8,128)(2,1)} %collective-permute-done.13.refs_2_, bf16[4,384,512]{2,1,0:T(8,128)(2,1)} %collective-permute-done.14.refs_3_, ...), custom_call_target="tpu_custom_call" | custom-call | flops 3221225472 | bytes 12582912 | tf_op jit(solution)/shard_map/pallas_call | solution.py:213
  194.7 3.6 shard_map.103
  198.3 5.2 %collective-permute-start.18 = (bf16[4,512,512]{2,1,0:T(8,128)(2,1)S(1)}, bf16[4,512,512]{2,1,0:T(8,128)(2,1)}, u32[]{:S(2)}, u32[]{:S(2)}) collective-permute-start(bf16[4,512,512]{2,1,0:T(8,128)(2,1)S(1)} %shard_map.103), channel_id=1, source_target_pairs={{0,1},{1,2},{2,3},{17,16},{18,17},{19,18},{4,5},{5,6},{6,7},{21,20... | collective-permute-start | bytes 6291464 | tf_op jit(solution)/shard_map/ppermute | solution.py:431
  203.5 10.7 %shard_map.94.refs_7_ = bf16[4,512,512]{2,1,0:T(8,128)(2,1)S(1)} custom-call(bf16[4,512,512]{2,1,0:T(8,128)(2,1)} %shard_map.92.refs_0_, bf16[4,512,512]{2,1,0:T(8,128)(2,1)} %collective-permute-done.9.refs_1_, bf16[4,512,512]{2,1,0:T(8,128)(2,1)} %collective-permute-done.10.refs_2_, bf16[4,512,512]{2,1,0:T(8,128)(2,1)} %collective-permute-done.11.refs_3_, ...), custom_call_target="tpu_custom_call" | custom-call | flops 4294967296 | bytes 16777216 | tf_op jit(solution)/shard_map/pallas_call | solution.py:213
  217.0 17.2 %shard_map.95 = (bf16[4,512,512]{2,1,0:T(8,128)(2,1)S(1)}, bf16[4,512,512]{2,1,0:T(8,128)(2,1)S(1)}) custom-call(bf16[4,512,512]{2,1,0:T(8,128)(2,1)} %shard_map.90.refs_0_, bf16[4,512,512]{2,1,0:T(8,128)(2,1)} %collective-permute-done.6.refs_1_, bf16[4,512,512]{2,1,0:T(8,128)(2,1)} %collective-permute-done.7.refs_2_, ...), custom_call_target="tpu_custom_call" | custom-call | flops 8589934592 | bytes 16777216 | tf_op jit(solution)/shard_map/pallas_call | solution.py:213
  234.3 4.3 %shard_map.87 = (bf16[4,512,512]{2,1,0:T(8,128)(2,1)}, bf16[4,512,512]{2,1,0:T(8,128)(2,1)}) custom-call(s32[5]{0:T(128)S(1)} %get-tuple-element.77.sc, bf16[4,4,512,512]{3,2,1,0:T(8,128)(2,1)} %bitcast.117), custom_call_target="tpu_custom_call" | custom-call | tf_op jit(solution)/shard_map/pallas_call | solution.py:130
  243.6 14.3 %shard_map.89 = (f32[4,512,512]{2,1,0:T(8,128)}, f32[4,512,512]{2,1,0:T(8,128)}) custom-call(bf16[4,384,512]{2,1,0:T(8,128)(2,1)S(1)} %copy-done.26, bf16[4,384,512]{2,1,0:T(8,128)(2,1)S(1)} %collective-permute-done.3.refs_1_, bf16[4,384,512]{2,1,0:T(8,128)(2,1)} %collective-permute-done.4.refs_2_, bf16[4,384,512]{2,1,0:T(8,128)(2,1)} %collective-permute-done.5.refs_3_, ...), custom_call_target="tpu_custom_call" | custom-call | flops 6442450944 | bytes 12582912 | tf_op jit(solution)/shard_map/pallas_call | solution.py:213
  261.2 12.0 %shard_map.101 = f32[4,512,512]{2,1,0:T(8,128)} custom-call(bf16[4,512,512]{2,1,0:T(8,128)(2,1)} %shard_map.92.refs_0_, bf16[4,512,512]{2,1,0:T(8,128)(2,1)} %collective-permute-done.9.refs_1_, bf16[4,512,512]{2,1,0:T(8,128)(2,1)} %collective-permute-done.10.refs_2_, bf16[4,512,512]{2,1,0:T(8,128)(2,1)} %collective-permute-done.11.refs_3_, ...), custom_call_target="tpu_custom_call" | custom-call | flops 4294967296 | bytes 16777216 | tf_op jit(solution)/shard_map/pallas_call | solution.py:213
  273.2 3.8 %add_convert_fusion.refs_0_ = bf16[4,512,512]{2,1,0:T(8,128)(2,1)S(1)} fusion(f32[4,512,512]{2,1,0:T(8,128)} %shard_map.101, bf16[4,512,512]{2,1,0:T(8,128)(2,1)} %collective-permute-done.18), kind=kLoop, calls=%fused_computation | loop fusion | flops 3145728 | bytes 8388608 | tf_op jit(solution)/shard_map/convert_element_type | solution.py:436
  277.6 11.4 %shard_map.99.refs_10_ = f32[4,512,512]{2,1,0:T(8,128)} custom-call(bf16[4,384,512]{2,1,0:T(8,128)(2,1)S(1)} %copy-done.6, bf16[4,384,512]{2,1,0:T(8,128)(2,1)S(1)} %copy-done.9, bf16[4,384,512]{2,1,0:T(8,128)(2,1)} %collective-permute-done.13.refs_2_, bf16[4,384,512]{2,1,0:T(8,128)(2,1)} %collective-permute-done.14.refs_3_, ...), custom_call_target="tpu_custom_call" | custom-call | flops 4294967296 | bytes 16777216 | tf_op jit(solution)/shard_map/pallas_call | solution.py:213
  292.1 8.5 %shard_map.100 = (bf16[4,512,512]{2,1,0:T(8,128)(2,1)S(1)}, bf16[4,512,512]{2,1,0:T(8,128)(2,1)S(1)}) custom-call(bf16[4,128,512]{2,1,0:T(8,128)(2,1)S(1)} %copy-done.21, bf16[4,128,512]{2,1,0:T(8,128)(2,1)S(1)} %collective-permute-done.refs_1_, bf16[4,128,512]{2,1,0:T(8,128)(2,1)S(1)} %collective-permute-done.1.refs_2_, ...), custom_call_target="tpu_custom_call" | custom-call | flops 2147483648 | bytes 4194304 | tf_op jit(solution)/shard_map/pallas_call | solution.py:213
  300.6 5.5 %shard_map.108.ready = bf16[2,4,512,512]{3,2,1,0:T(8,128)(2,1)S(1)} custom-call(s32[1]{0:T(128)} %bitcast.22.flag, bf16[4,512,512]{2,1,0:T(8,128)(2,1)} %collective-permute-done.24.other, bf16[512,512]{1,0:T(8,128)(2,1)S(1)} %copy-done.28, bf16[512,512]{1,0:T(8,128)(2,1)} %collective-permute-done.25.theirs), custom_call_target="tpu_custom_call" | custom-call | flops 2147483648 | bytes 6291456 | tf_op jit(solution)/shard_map/pallas_call | solution.py:253
  318.2 4.2 %collective-permute-done.27 = bf16[1,128,512]{2,1,0:T(8,128)(2,1)S(1)} collective-permute-done((bf16[1,128,512]{2,1,0:T(8,128)(2,1)S(1)}, bf16[1,128,512]{2,1,0:T(8,128)(2,1)S(1)}, u32[]{:S(2)}, u32[]{:S(2)}) %collective-permute-start.27) | collective-permute-done | bytes 131104 | tf_op jit(solution)/shard_map/ppermute | solution.py:335
  322.8 27.3 %collective-permute-done.20.theirs = bf16[512,512]{1,0:T(8,128)(2,1)S(1)} collective-permute-done((bf16[512,512]{1,0:T(8,128)(2,1)}, bf16[512,512]{1,0:T(8,128)(2,1)S(1)}, u32[]{:S(2)}, u32[]{:S(2)}) %collective-permute-start.20) | collective-permute-done | bytes 524320 | tf_op jit(solution)/shard_map/ppermute | solution.py:335
  350.1 3.8 %shard_map.106.ready = bf16[2,4,512,512]{3,2,1,0:T(8,128)(2,1)S(1)} custom-call(s32[1]{0:T(128)} %bitcast.22.flag, bf16[4,512,512]{2,1,0:T(8,128)(2,1)S(1)} %collective-permute-done.19.other, bf16[512,512]{1,0:T(8,128)(2,1)S(1)} %copy-done.27, bf16[512,512]{1,0:T(8,128)(2,1)S(1)} %collective-permute-done.20.theirs), custom_call_target="tpu_custom_call" | custom-call | flops 2147483648 | bytes 6291456 | tf_op jit(solution)/shard_map/pallas_call | solution.py:253
  360.7 4.2 %collective-permute-done.22 = bf16[1,128,512]{2,1,0:T(8,128)(2,1)S(1)} collective-permute-done((bf16[1,128,512]{2,1,0:T(8,128)(2,1)S(1)}, bf16[1,128,512]{2,1,0:T(8,128)(2,1)S(1)}, u32[]{:S(2)}, u32[]{:S(2)}) %collective-permute-start.22) | collective-permute-done | bytes 131104 | tf_op jit(solution)/shard_map/ppermute | solution.py:335
  366.8 3.2 collective-permute-done.23
  (185 shorter events, 69.2 us)
Async XLA Ops:
  1.7 15.9 %collective-permute-start.16 = (bf16[4,128,512]{2,1,0:T(8,128)(2,1)S(1)}, bf16[4,128,512]{2,1,0:T(8,128)(2,1)}, u32[]{:S(2)}, u32[]{:S(2)}) collective-permute-start(bf16[4,128,512]{2,1,0:T(8,128)(2,1)S(1)} %shard_map.97.refs_4_.refs_0_), channel_id=1, source_target_pairs={{0,8},{4,12},{8,0},{12,4},{1,9},{5,13},{9,1},{13,5},{2,10},{6,14},... | collective-permute-start | bytes 1572872 | tf_op jit(solution)/shard_map/ppermute | solution.py:335
  7.7 89.2 %collective-permute-start.10 = (bf16[4,512,512]{2,1,0:T(8,128)(2,1)}, bf16[4,512,512]{2,1,0:T(8,128)(2,1)}, u32[]{:S(2)}, u32[]{:S(2)}) collective-permute-start(bf16[4,512,512]{2,1,0:T(8,128)(2,1)} %shard_map.92.refs_0_), channel_id=1, source_target_pairs={{0,8},{4,12},{8,0},{12,4},{1,9},{5,13},{9,1},{13,5},{2,10},{6,14},... | collective-permute-start | bytes 6291464 | tf_op jit(solution)/shard_map/ppermute | solution.py:335
  9.3 87.0 %collective-permute-start.13 = (bf16[4,384,512]{2,1,0:T(8,128)(2,1)S(1)}, bf16[4,384,512]{2,1,0:T(8,128)(2,1)}, u32[]{:S(2)}, u32[]{:S(2)}) collective-permute-start(bf16[4,384,512]{2,1,0:T(8,128)(2,1)S(1)} %shard_map.96.refs_0_), channel_id=1, source_target_pairs={{0,8},{4,12},{8,0},{12,4},{1,9},{5,13},{9,1},{13,5},{2,10},{6,14},... | collective-permute-start | bytes 4718600 | tf_op jit(solution)/shard_map/ppermute | solution.py:335
  11.3 11.4 %collective-permute-start.15 = (bf16[4,128,512]{2,1,0:T(8,128)(2,1)S(1)}, bf16[4,128,512]{2,1,0:T(8,128)(2,1)S(1)}, u32[]{:S(2)}, u32[]{:S(2)}) collective-permute-start(bf16[4,128,512]{2,1,0:T(8,128)(2,1)S(1)} %shard_map.97.refs_4_.refs_0_), channel_id=1, source_target_pairs={{0,4},{4,0},{8,12},{12,8},{1,5},{5,1},{9,13},{13,9},{2,6},{6,2},{1... | collective-permute-start | bytes 1572872 | tf_op jit(solution)/shard_map/ppermute | solution.py:335
  20.6 153.5 %collective-permute-start.7 = (bf16[4,512,512]{2,1,0:T(8,128)(2,1)}, bf16[4,512,512]{2,1,0:T(8,128)(2,1)}, u32[]{:S(2)}, u32[]{:S(2)}) collective-permute-start(bf16[4,512,512]{2,1,0:T(8,128)(2,1)} %shard_map.90.refs_0_), channel_id=1, source_target_pairs={{0,8},{4,12},{8,0},{12,4},{1,9},{5,13},{9,1},{13,5},{2,10},{6,14},... | collective-permute-start | bytes 6291464 | tf_op jit(solution)/shard_map/ppermute | solution.py:335
  23.5 74.1 %collective-permute-start.12 = (bf16[4,384,512]{2,1,0:T(8,128)(2,1)S(1)}, bf16[4,384,512]{2,1,0:T(8,128)(2,1)S(1)}, u32[]{:S(2)}, u32[]{:S(2)}) collective-permute-start(bf16[4,384,512]{2,1,0:T(8,128)(2,1)S(1)} %shard_map.96.refs_0_), channel_id=1, source_target_pairs={{0,4},{4,0},{8,12},{12,8},{1,5},{5,1},{9,13},{13,9},{2,6},{6,2},{1... | collective-permute-start | bytes 4718600 | tf_op jit(solution)/shard_map/ppermute | solution.py:335
  26.3 147.7 %collective-permute-start.4 = (bf16[4,384,512]{2,1,0:T(8,128)(2,1)}, bf16[4,384,512]{2,1,0:T(8,128)(2,1)}, u32[]{:S(2)}, u32[]{:S(2)}) collective-permute-start(bf16[4,384,512]{2,1,0:T(8,128)(2,1)} %copy-done.25), channel_id=1, source_target_pairs={{0,8},{4,12},{8,0},{12,4},{1,9},{5,13},{9,1},{13,5},{2,10},{6,14},... | collective-permute-start | bytes 4718600 | tf_op jit(solution)/shard_map/ppermute | solution.py:335
  96.3 81.8 %collective-permute-start.9 = (bf16[4,512,512]{2,1,0:T(8,128)(2,1)}, bf16[4,512,512]{2,1,0:T(8,128)(2,1)}, u32[]{:S(2)}, u32[]{:S(2)}) collective-permute-start(bf16[4,512,512]{2,1,0:T(8,128)(2,1)} %shard_map.92.refs_0_), channel_id=1, source_target_pairs={{0,4},{4,0},{8,12},{12,8},{1,5},{5,1},{9,13},{13,9},{2,6},{6,2},{1... | collective-permute-start | bytes 6291464 | tf_op jit(solution)/shard_map/ppermute | solution.py:335
  96.9 101.4 %collective-permute-start.11 = (bf16[4,512,512]{2,1,0:T(8,128)(2,1)}, bf16[4,512,512]{2,1,0:T(8,128)(2,1)}, u32[]{:S(2)}, u32[]{:S(2)}) collective-permute-start(bf16[4,512,512]{2,1,0:T(8,128)(2,1)} %collective-permute-done.10.refs_2_), channel_id=1, source_target_pairs={{0,4},{4,0},{8,12},{12,8},{1,5},{5,1},{9,13},{13,9},{2,6},{6,2},{1... | collective-permute-start | bytes 6291464 | tf_op jit(solution)/shard_map/ppermute | solution.py:335
  97.6 80.5 %collective-permute-start.14 = (bf16[4,384,512]{2,1,0:T(8,128)(2,1)}, bf16[4,384,512]{2,1,0:T(8,128)(2,1)}, u32[]{:S(2)}, u32[]{:S(2)}) collective-permute-start(bf16[4,384,512]{2,1,0:T(8,128)(2,1)} %collective-permute-done.13.refs_2_), channel_id=1, source_target_pairs={{0,4},{4,0},{8,12},{12,8},{1,5},{5,1},{9,13},{13,9},{2,6},{6,2},{1... | collective-permute-start | bytes 4718600 | tf_op jit(solution)/shard_map/ppermute | solution.py:335
  174.1 41.4 %collective-permute-start.6 = (bf16[4,512,512]{2,1,0:T(8,128)(2,1)}, bf16[4,512,512]{2,1,0:T(8,128)(2,1)}, u32[]{:S(2)}, u32[]{:S(2)}) collective-permute-start(bf16[4,512,512]{2,1,0:T(8,128)(2,1)} %shard_map.90.refs_0_), channel_id=1, source_target_pairs={{0,4},{4,0},{8,12},{12,8},{1,5},{5,1},{9,13},{13,9},{2,6},{6,2},{1... | collective-permute-start | bytes 6291464 | tf_op jit(solution)/shard_map/ppermute | solution.py:335
  174.1 42.9 %collective-permute-start.8 = (bf16[4,512,512]{2,1,0:T(8,128)(2,1)}, bf16[4,512,512]{2,1,0:T(8,128)(2,1)}, u32[]{:S(2)}, u32[]{:S(2)}) collective-permute-start(bf16[4,512,512]{2,1,0:T(8,128)(2,1)} %collective-permute-done.7.refs_2_), channel_id=1, source_target_pairs={{0,4},{4,0},{8,12},{12,8},{1,5},{5,1},{9,13},{13,9},{2,6},{6,2},{1... | collective-permute-start | bytes 6291464 | tf_op jit(solution)/shard_map/ppermute | solution.py:335
  178.0 60.7 %collective-permute-start.3 = (bf16[4,384,512]{2,1,0:T(8,128)(2,1)}, bf16[4,384,512]{2,1,0:T(8,128)(2,1)S(1)}, u32[]{:S(2)}, u32[]{:S(2)}) collective-permute-start(bf16[4,384,512]{2,1,0:T(8,128)(2,1)} %copy-done.25), channel_id=1, source_target_pairs={{0,4},{4,0},{8,12},{12,8},{1,5},{5,1},{9,13},{13,9},{2,6},{6,2},{1... | collective-permute-start | bytes 4718600 | tf_op jit(solution)/shard_map/ppermute | solution.py:335
  178.1 62.2 %collective-permute-start.5 = (bf16[4,384,512]{2,1,0:T(8,128)(2,1)}, bf16[4,384,512]{2,1,0:T(8,128)(2,1)}, u32[]{:S(2)}, u32[]{:S(2)}) collective-permute-start(bf16[4,384,512]{2,1,0:T(8,128)(2,1)} %collective-permute-done.4.refs_2_), channel_id=1, source_target_pairs={{0,4},{4,0},{8,12},{12,8},{1,5},{5,1},{9,13},{13,9},{2,6},{6,2},{1... | collective-permute-start | bytes 4718600 | tf_op jit(solution)/shard_map/ppermute | solution.py:335
  198.3 74.8 %collective-permute-start.18 = (bf16[4,512,512]{2,1,0:T(8,128)(2,1)S(1)}, bf16[4,512,512]{2,1,0:T(8,128)(2,1)}, u32[]{:S(2)}, u32[]{:S(2)}) collective-permute-start(bf16[4,512,512]{2,1,0:T(8,128)(2,1)S(1)} %shard_map.103), channel_id=1, source_target_pairs={{0,1},{1,2},{2,3},{17,16},{18,17},{19,18},{4,5},{5,6},{6,7},{21,20... | collective-permute-start | bytes 6291464 | tf_op jit(solution)/shard_map/ppermute | solution.py:431
  215.5 23.2 %collective-permute-start.1 = (bf16[4,128,512]{2,1,0:T(8,128)(2,1)S(1)}, bf16[4,128,512]{2,1,0:T(8,128)(2,1)S(1)}, u32[]{:S(2)}, u32[]{:S(2)}) collective-permute-start(bf16[4,128,512]{2,1,0:T(8,128)(2,1)S(1)} %copy-done.21), channel_id=1, source_target_pairs={{0,8},{4,12},{8,0},{12,4},{1,9},{5,13},{9,1},{13,5},{2,10},{6,14},... | collective-permute-start | bytes 1572872 | tf_op jit(solution)/shard_map/ppermute | solution.py:335
  234.2 66.4 %collective-permute-start.24 = (bf16[4,512,512]{2,1,0:T(8,128)(2,1)S(1)}, bf16[4,512,512]{2,1,0:T(8,128)(2,1)}, u32[]{:S(2)}, u32[]{:S(2)}) collective-permute-start(bf16[4,512,512]{2,1,0:T(8,128)(2,1)S(1)} %get-tuple-element.37.refs_1_), channel_id=1, source_target_pairs={{0,16},{16,0},{1,17},{17,1},{2,18},{18,2},{3,19},{19,3},{4,20},{20... | collective-permute-start | bytes 6291464 | tf_op jit(solution)/shard_map/ppermute | solution.py:335
  238.7 50.3 %collective-permute-start = (bf16[4,128,512]{2,1,0:T(8,128)(2,1)S(1)}, bf16[4,128,512]{2,1,0:T(8,128)(2,1)S(1)}, u32[]{:S(2)}, u32[]{:S(2)}) collective-permute-start(bf16[4,128,512]{2,1,0:T(8,128)(2,1)S(1)} %copy-done.21), channel_id=1, source_target_pairs={{0,4},{4,0},{8,12},{12,8},{1,5},{5,1},{9,13},{13,9},{2,6},{6,2},{1... | collective-permute-start | bytes 1572872 | tf_op jit(solution)/shard_map/ppermute | solution.py:335
  238.8 61.8 %collective-permute-start.25 = (bf16[512,512]{1,0:T(8,128)(2,1)}, bf16[512,512]{1,0:T(8,128)(2,1)}, u32[]{:S(2)}, u32[]{:S(2)}) collective-permute-start(bf16[512,512]{1,0:T(8,128)(2,1)} %get-tuple-element.62), channel_id=1, source_target_pairs={{0,16},{16,0},{1,17},{17,1},{2,18},{18,2},{3,19},{19,3},{4,20},{20... | collective-permute-start | bytes 1572872 | tf_op jit(solution)/shard_map/ppermute | solution.py:335
  240.3 50.2 %collective-permute-start.2 = (bf16[4,128,512]{2,1,0:T(8,128)(2,1)S(1)}, bf16[4,128,512]{2,1,0:T(8,128)(2,1)}, u32[]{:S(2)}, u32[]{:S(2)}) collective-permute-start(bf16[4,128,512]{2,1,0:T(8,128)(2,1)S(1)} %collective-permute-done.1.refs_2_), channel_id=1, source_target_pairs={{0,4},{4,0},{8,12},{12,8},{1,5},{5,1},{9,13},{13,9},{2,6},{6,2},{1... | collective-permute-start | bytes 1572872 | tf_op jit(solution)/shard_map/ppermute | solution.py:335
  276.9 73.1 %collective-permute-start.19 = (bf16[4,512,512]{2,1,0:T(8,128)(2,1)S(1)}, bf16[4,512,512]{2,1,0:T(8,128)(2,1)S(1)}, u32[]{:S(2)}, u32[]{:S(2)}) collective-permute-start(bf16[4,512,512]{2,1,0:T(8,128)(2,1)S(1)} %add_convert_fusion.refs_0_), channel_id=1, source_target_pairs={{0,16},{16,0},{1,17},{17,1},{2,18},{18,2},{3,19},{19,3},{4,20},{20... | collective-permute-start | bytes 6291464 | tf_op jit(solution)/shard_map/ppermute | solution.py:335
  289.0 61.1 %collective-permute-start.20 = (bf16[512,512]{1,0:T(8,128)(2,1)}, bf16[512,512]{1,0:T(8,128)(2,1)S(1)}, u32[]{:S(2)}, u32[]{:S(2)}) collective-permute-start(bf16[512,512]{1,0:T(8,128)(2,1)} %get-tuple-element.63), channel_id=1, source_target_pairs={{0,16},{16,0},{1,17},{17,1},{2,18},{18,2},{3,19},{19,3},{4,20},{20... | collective-permute-start | bytes 1572872 | tf_op jit(solution)/shard_map/ppermute | solution.py:335
  317.1 38.8 %collective-permute-start.30 = (bf16[1,128,512]{2,1,0:T(8,128)(2,1)S(1)}, bf16[1,128,512]{2,1,0:T(8,128)(2,1)S(1)}, u32[]{:S(2)}, u32[]{:S(2)}) collective-permute-start(bf16[1,128,512]{2,1,0:T(8,128)(2,1)S(1)} %fusion.22), channel_id=1, source_target_pairs={{0,8},{4,12},{8,0},{12,4},{1,9},{5,13},{9,1},{13,5},{2,10},{6,14},... | collective-permute-start | bytes 393224 | tf_op jit(solution)/shard_map/ppermute | solution.py:335
  322.4 44.4 %collective-permute-start.28 = (bf16[128,512]{1,0:T(8,128)(2,1)S(1)}, bf16[128,512]{1,0:T(8,128)(2,1)S(1)}, u32[]{:S(2)}, u32[]{:S(2)}) collective-permute-start(bf16[128,512]{1,0:T(8,128)(2,1)S(1)} %fusion.19), channel_id=1, source_target_pairs={{0,16},{16,0},{1,17},{17,1},{2,18},{18,2},{3,19},{19,3},{4,20},{20... | collective-permute-start | bytes 393224 | tf_op jit(solution)/shard_map/ppermute | solution.py:335
  (44 other events, 366.5 us)
